TPU v7x, 768 devices: a whole 4x8x12 slice. The times are simulated.
768 devices in a mesh: curve: 96 (over x, z, core), tile: 8 (over y).
Axes of the slice: x: 4, y: 8, z: 12, core: 2. Of those that a mesh axis runs over, the one named last changes fastest.
Arguments:
- state: float32 [5, 24576, 512], P(None, ('curve', 'tile')), may hold values from -6 to 6
- levels: int32 [24576], P(('curve', 'tile')), may hold values from 0 to 2
- send_faces: int32 [6144, 2], P(('curve', 'tile')), may hold values from 0 to 959, as said below
- send_counts: int32 [6144], P(('curve', 'tile')), may hold values from 0 to 2, as said below
- recv_faces: int32 [6144, 2], P(('curve', 'tile')), may hold values from 0 to 191, as said below
- recv_orients: int32 [6144, 2], P(('curve', 'tile')), may hold values from 0 to 7, as said below
- recv_counts: int32 [6144], P(('curve', 'tile')), may hold values from 0 to 2
- curve_faces: int32 [1536, 16], P(('curve', 'tile')), may hold values from 0 to 191, as said below
- curve_orients: int32 [1536, 16], P(('curve', 'tile')), may hold values from 0 to 7, as said below
- curve_counts: int32 [1536], P(('curve', 'tile')), may hold values from 0 to 16, as said below
Outputs:
- advanced: float32 [5, 24576, 512], P(None, ('curve', 'tile'))
Inputs may be any that keep to these rules, and one draw needn't show every extreme that they name: `send_faces`: row p of device (b, t) lists in its first send_counts entries the pairs it shares with device (b, p): (6 e + f) 5 + c with f 3 or 5 and c 0 to 3 for a half-face mortar of a coarse face, 4 for a whole face; each coarse face listed has its four children 0 to 3 listed once each, possibly with different peers; any other face id appears at most once in all lists of a device; entries past the count are 0. `send_counts`: the count of device (b, t) for peer p equals the receive count of device (b, p) for peer t. `recv_faces`: slot k of row t of device (b, p) is face 6 e + f paired with slot k of row p of device (b, t), with f = 2 where the sender's face is 3 and 4 where it is 5; entries past the count are 0. `recv_orients`: R_o maps the sender's node order into the receiver's; 0 past the count. `curve_faces`: row 0 names faces with f = 0, row 1 faces with f = 1; slot k of row 1 of device (b, t) pairs with slot k of row 0 of device (b + 1, t); entries past the count are 0. `curve_orients`: the two sides of a pair hold mutually inverse orientations; 0 past the count. `curve_counts`: both sides of a pair of rows hold the same count; it is 0 towards a curve index that does not exist.
All inputs are finite; a program needn't handle non-finite values.
Results may differ from a plain program's by a relative error of at most 0.0003.
Values sent between devices are 32-bit elements; how exact they have to be, the bound alone decides.
No kernel may reach another device: no remote copies, remote signals or barrier semaphores. Data moves between devices by JAX's collectives and lax.ppermute only.
A program may use at most 64 MiB of HBM per device.

v0:
```python
import jax
import jax.numpy as jnp
import numpy as np
from jax import lax
from jax.sharding import PartitionSpec as P

time_step = 0.002
wave_speed = 1.0
highest = lax.Precision.HIGHEST
inner_nodes = [
    -0.8717401485096066,
    -0.5917001814331423,
    -0.20929921790247888,
    0.20929921790247888,
    0.5917001814331423,
    0.8717401485096066,
]


def from_behind(block, axis, distance):
    devices = range(lax.axis_size(axis))
    route = [(i - distance, i) for i in devices if i - distance in devices]
    return lax.ppermute(block, axis, route)


def legendre_seven(abscissa):
    before = abscissa * 0.0 + 1.0
    current = abscissa + 0.0
    for order in range(1, 7):
        before, current = (
            current,
            ((2 * order + 1) * abscissa * current - order * before) / (order + 1),
        )
    return current


def basis_tables():
    degree = 7
    points = np.array([-1.0] + inner_nodes + [1.0])
    values = legendre_seven(points)
    weights = 2.0 / (degree * (degree + 1) * values**2)
    deriv_mat = np.zeros((8, 8))
    for row_at in range(8):
        for col_at in range(8):
            if row_at != col_at:
                deriv_mat[row_at, col_at] = values[row_at] / (
                    values[col_at] * (points[row_at] - points[col_at])
                )
    deriv_mat[0, 0] = -degree * (degree + 1) / 4.0
    deriv_mat[7, 7] = degree * (degree + 1) / 4.0
    halves = []
    projections = []
    for half_side in range(2):
        targets = (points + 2.0 * half_side - 1.0) / 2.0
        interp = np.ones((8, 8))
        for col_at in range(8):
            for other_at in range(8):
                if other_at != col_at:
                    interp[:, col_at] *= (targets - points[other_at]) / (
                        points[col_at] - points[other_at]
                    )
        halves.append(interp)
        projections.append(0.5 * (interp.T * weights[None, :]) / weights[:, None])
    interp_mats = np.stack(
        [
            np.kron(halves[first_at], halves[second_at])
            for first_at in range(2)
            for second_at in range(2)
        ]
        + [np.eye(64)]
    )
    proj_mats = np.stack(
        [
            np.kron(projections[first_at], projections[second_at])
            for first_at in range(2)
            for second_at in range(2)
        ]
        + [np.eye(64)]
    )
    perm_table = np.zeros((8, 64), np.int32)
    for orient_code in range(8):
        for first_at in range(8):
            for second_at in range(8):
                if orient_code & 4:
                    upper_at, lower_at = (second_at, first_at)
                else:
                    upper_at, lower_at = (first_at, second_at)
                if orient_code & 1:
                    upper_at = 7 - upper_at
                if orient_code & 2:
                    lower_at = 7 - lower_at
                perm_table[orient_code, 8 * first_at + second_at] = 8 * upper_at + lower_at
    inverse_table = np.argsort(perm_table, axis=1).astype(np.int32)
    deriv_first = np.kron(deriv_mat, np.eye(64))
    deriv_second = np.kron(np.eye(8), np.kron(deriv_mat, np.eye(8)))
    deriv_third = np.kron(np.eye(64), deriv_mat)
    selector = np.zeros((512, 384))
    for first_at in range(8):
        for second_at in range(8):
            column = 8 * first_at + second_at
            for side_at in range(2):
                edge = 7 * side_at
                selector[64 * edge + 8 * first_at + second_at, 64 * side_at + column] = 1.0
                selector[64 * first_at + 8 * edge + second_at, 64 * (2 + side_at) + column] = 1.0
                selector[64 * first_at + 8 * second_at + edge, 64 * (4 + side_at) + column] = 1.0
    lift_end = float(1.0 / weights[0])
    return (
        jnp.asarray(interp_mats, jnp.float32),
        jnp.asarray(proj_mats, jnp.float32),
        jnp.asarray(perm_table, jnp.int32),
        jnp.asarray(inverse_table, jnp.int32),
        lift_end,
        jnp.asarray(deriv_first, jnp.float32),
        jnp.asarray(deriv_second, jnp.float32),
        jnp.asarray(deriv_third, jnp.float32),
        jnp.asarray(selector, jnp.float32),
    )


def face_traces(current, selector):
    fields, elements, npoints = current.shape
    flat = jnp.dot(current.reshape(fields * elements, npoints), selector, precision=highest)
    return flat.reshape(fields, elements * 6, 64)


def spread_faces(jump_term, elements, selector):
    fields = jump_term.shape[0]
    flat = jnp.dot(jump_term.reshape(fields * elements, 384), selector.T, precision=highest)
    return flat.reshape(fields, elements, 512)


def dim_picks(face_ids):
    return ((face_ids % 6 // 2)[None, :] == jnp.arange(3, dtype=jnp.int32)[:, None]).astype(
        jnp.float32
    )


def normal_flux(trace_set, face_ids):
    pick_mask = dim_picks(face_ids)
    sign_vals = (face_ids % 2 * 2 - 1).astype(jnp.float32)[:, None]
    normal_vel = jnp.sum(pick_mask[:, :, None] * trace_set[1:4], axis=0)
    pressure = sign_vals * trace_set[4]
    return jnp.stack(
        [
            sign_vals * normal_vel,
            pick_mask[0][:, None] * pressure,
            pick_mask[1][:, None] * pressure,
            pick_mask[2][:, None] * pressure,
            sign_vals * normal_vel,
        ]
    )


def wall_state(own_side, face_ids):
    flip_vals = 1.0 - 2.0 * dim_picks(face_ids)
    return jnp.concatenate(
        [own_side[:1], own_side[1:4] * flip_vals[:, :, None], own_side[4:]], axis=0
    )


def rusanov(own_side, other_side, face_ids):
    average = 0.5 * (normal_flux(own_side, face_ids) + normal_flux(other_side, face_ids))
    return average - 0.5 * wave_speed * (other_side - own_side)


def orient(values, orient_codes, lookup):
    matches = (orient_codes[:, None] == jnp.arange(8, dtype=jnp.int32)[None, :]).astype(jnp.int32)
    gather_index = jnp.sum(matches[:, :, None] * lookup[None, :, :], axis=1)
    return jnp.take_along_axis(values, jnp.broadcast_to(gather_index[None], values.shape), axis=2)


def child_apply(values, child_ids, matrices):
    mapped = jnp.einsum("fnj,cij->cfni", values, matrices, precision=highest)
    pick_mask = (child_ids[None, :] == jnp.arange(5, dtype=jnp.int32)[:, None]).astype(jnp.float32)
    return jnp.sum(pick_mask[:, None, :, None] * mapped, axis=0)


def volume_term(current, deriv_first, deriv_second, deriv_third):
    fields, elements, npoints = current.shape
    grad_x = jnp.dot(
        current[1:5:3].reshape(2 * elements, 512), deriv_first.T, precision=highest
    ).reshape(2, elements, 512)
    grad_y = jnp.dot(
        current[2:5:2].reshape(2 * elements, 512), deriv_second.T, precision=highest
    ).reshape(2, elements, 512)
    grad_z = jnp.dot(
        current[3:5].reshape(2 * elements, 512), deriv_third.T, precision=highest
    ).reshape(2, elements, 512)
    diverge = grad_x[0] + grad_y[0] + grad_z[0]
    return -jnp.stack([diverge, grad_x[1], grad_y[1], grad_z[1], diverge])


def shards(
    state,
    levels,
    send_faces,
    send_counts,
    recv_faces,
    recv_orients,
    recv_counts,
    curve_faces,
    curve_orients,
    curve_counts,
):
    (
        interp_mats,
        proj_mats,
        perm_table,
        inverse_table,
        lift_end,
        deriv_first,
        deriv_second,
        deriv_third,
        selector,
    ) = basis_tables()
    fields, elements, npoints = state.shape
    face_total = elements * 6
    tile_total, slot_total = send_faces.shape
    rim_slots = curve_faces.shape[1]
    block_width = slot_total * 64
    scales = jnp.exp2(levels.astype(jnp.float32))
    face_scales = jnp.repeat(scales, 6) * lift_end
    slot_range = jnp.arange(slot_total, dtype=jnp.int32)
    send_live = slot_range[None, :] < send_counts[:, None]
    send_ids = jnp.where(send_live, send_faces // 5, face_total).reshape(-1)
    child_ids = (send_faces % 5).reshape(-1)
    send_mask = send_live.reshape(-1).astype(jnp.float32)[None, :, None]
    recv_live = slot_range[None, :] < recv_counts[:, None]
    recv_ids = jnp.where(recv_live, recv_faces, face_total).reshape(-1)
    recv_codes = recv_orients.reshape(-1)
    recv_mask = recv_live.reshape(-1).astype(jnp.float32)[None, :, None]
    curve_live = jnp.arange(rim_slots, dtype=jnp.int32)[None, :] < curve_counts[:, None]
    curve_ids = jnp.where(curve_live, curve_faces, face_total).reshape(-1)
    curve_codes = curve_orients.reshape(-1)
    curve_mask = curve_live.reshape(-1).astype(jnp.float32)[None, :, None]
    all_faces = jnp.arange(face_total, dtype=jnp.int32)

    def rhs(current):
        traces = face_traces(current, selector)
        padded = jnp.concatenate([traces, jnp.zeros((fields, 1, 64), jnp.float32)], axis=1)
        mortar = child_apply(padded[:, send_ids], child_ids, interp_mats) * send_mask
        own_recv = padded[:, recv_ids]
        own_curve = padded[:, curve_ids]
        arrived = lax.all_to_all(
            mortar.reshape(fields, tile_total, block_width),
            "tile",
            split_axis=1,
            concat_axis=1,
            tiled=True,
        )
        fine_flux = (
            rusanov(
                own_recv, orient(arrived.reshape(fields, -1, 64), recv_codes, perm_table), recv_ids
            )
            * recv_mask
        )
        returned = orient(fine_flux, recv_codes, inverse_table).reshape(
            fields, tile_total, block_width
        )
        coarse_flux = (
            -lax.all_to_all(returned, "tile", split_axis=1, concat_axis=1, tiled=True).reshape(
                fields, -1, 64
            )
            * send_mask
        )
        rightward = own_curve[:, rim_slots:].reshape(fields, rim_slots * 64)
        from_left = from_behind(rightward, "curve", 1).reshape(fields, rim_slots, 64)
        left_flux = (
            rusanov(
                own_curve[:, :rim_slots],
                orient(from_left, curve_codes[:rim_slots], perm_table),
                curve_ids[:rim_slots],
            )
            * curve_mask[:, :rim_slots]
        )
        answered = orient(left_flux, curve_codes[:rim_slots], inverse_table).reshape(
            fields, rim_slots * 64
        )
        right_flux = (
            -from_behind(answered, "curve", -1).reshape(fields, rim_slots, 64)
            * curve_mask[:, rim_slots:]
        )
        curve_flux = jnp.concatenate([left_flux, right_flux], axis=1)
        accumulated = jnp.zeros((fields, face_total + 1, 64), jnp.float32)
        accumulated = accumulated.at[:, send_ids].add(
            child_apply(coarse_flux, child_ids, proj_mats)
        )
        accumulated = accumulated.at[:, recv_ids].add(fine_flux)
        accumulated = accumulated.at[:, curve_ids].add(curve_flux)
        listed = jnp.zeros((face_total + 1,), jnp.float32)
        listed = listed.at[send_ids].add(1.0).at[recv_ids].add(1.0).at[curve_ids].add(1.0)
        wall_flux = rusanov(traces, wall_state(traces, all_faces), all_faces)
        flux_star = jnp.where(
            listed[None, :face_total, None] > 0.0, accumulated[:, :face_total], wall_flux
        )
        jump_term = (normal_flux(traces, all_faces) - flux_star) * face_scales[None, :, None]
        volume = volume_term(current, deriv_first, deriv_second, deriv_third)
        return volume * scales[None, :, None] + spread_faces(jump_term, elements, selector)

    section_one = state + time_step * rhs(state)
    section_two = 0.75 * state + 0.25 * (section_one + time_step * rhs(section_one))
    return state / 3.0 + 2.0 / 3.0 * (section_two + time_step * rhs(section_two))


def solution(mesh):
    return jax.shard_map(
        shards,
        mesh=mesh,
        in_specs=(
            P(None, ("curve", "tile"), None),
            P(("curve", "tile")),
            P(("curve", "tile"), None),
            P(("curve", "tile")),
            P(("curve", "tile"), None),
            P(("curve", "tile"), None),
            P(("curve", "tile")),
            P(("curve", "tile"), None),
            P(("curve", "tile"), None),
            P(("curve", "tile")),
        ),
        out_specs=P(None, ("curve", "tile"), None),
        check_vma=False,
    )
```

profile of v0, /device:TPU:6, one launch (start us, length us, event | category | flops | bytes accessed | tf_op | source)
XLA Modules:
  0.0 870.8 jit_solution(1106417326089973827)
XLA Ops:
  10.9 7.1 all-to-all-start
  29.7 2.1 convolution_bitcast_fusion.7
  50.2 64.6 %gather_fusion.11 = f32[5120]{0:T(1024)} fusion(f32[5,16,64]{2,1,0:T(8,128)S(1)} %reshape.2066, s32[5120]{0:T(1024)S(1)} %reshape.2413), kind=kCustom, calls=%fused_computation.2.clone | custom fusion | bytes 102400 | tf_op jit(solution)/shard_map/jit(take_along_axis)/gather | solution.py:169
  117.4 42.8 %gather_fusion.12 = f32[5120]{0:T(1024)S(1)} fusion(f32[5,16,64]{2,1,0:T(8,128)S(1)} %fusion.60, s32[5120]{0:T(1024)S(1)} %reshape.2418), kind=kCustom, calls=%fused_computation.3.clone | custom fusion | bytes 102400 | tf_op jit(solution)/shard_map/jit(take_along_axis)/gather | solution.py:169
  161.0 14.0 %collective-permute-start.1 = (f32[5,1024]{1,0:T(8,128)}, f32[5,1024]{1,0:T(8,128)}, u32[]{:S(2)}, u32[]{:S(2)}) collective-permute-start(f32[5,1024]{1,0:T(8,128)} %reshape.2067), channel_id=1, source_target_pairs={{8,0},{16,8},{24,16},{32,24},{40,32},{48,40},{56,48},{64,56},{72,6... | collective-permute-start | bytes 61448 | tf_op jit(solution)/shard_map/ppermute | solution.py:23
  175.9 42.8 %gather_fusion.9 = f32[5120]{0:T(1024)S(1)} fusion(f32[5,16,64]{2,1,0:T(8,128)S(1)} %reshape.2063, s32[5120]{0:T(1024)S(1)} %reshape.2403), kind=kCustom, calls=%fused_computation.clone | custom fusion | bytes 102400 | tf_op jit(solution)/shard_map/jit(take_along_axis)/gather | solution.py:169
  222.8 64.6 %gather_fusion.10 = f32[5120]{0:T(1024)} fusion(f32[5,16,64]{2,1,0:T(8,128)S(1)} %subtract_multiply_fusion.2, s32[5120]{0:T(1024)S(1)} %reshape.2408), kind=kCustom, calls=%fused_computation.1.clone | custom fusion | bytes 102400 | tf_op jit(solution)/shard_map/jit(take_along_axis)/gather | solution.py:169
  293.0 7.4 all-to-all-start.1
  304.2 4.4 all-to-all-done.1
  314.3 2.4 scatter_fusion.2
  316.7 2.6 scatter_fusion.3
  319.3 3.9 scatter_fusion.4
  323.2 2.1 slice.620
  325.3 2.1 copy.527
  327.4 2.2 fusion.26
  329.5 2.0 copy.476
  333.5 2.4 fusion.1
  340.7 2.5 gather_fusion.5
  343.1 2.4 gather_fusion.4
  346.2 2.1 fusion.125
  377.0 3.9 all-to-all-start.2
  384.8 42.8 %gather_fusion.15 = f32[5120]{0:T(1024)S(1)} fusion(f32[5,16,64]{2,1,0:T(8,128)S(1)} %reshape.2076, s32[5120]{0:T(1024)S(1)} %reshape.2413), kind=kCustom, calls=%fused_computation.6.clone | custom fusion | bytes 102400 | tf_op jit(solution)/shard_map/jit(take_along_axis)/gather | solution.py:169
  429.2 42.8 %gather_fusion.16 = f32[5120]{0:T(1024)S(1)} fusion(f32[5,16,64]{2,1,0:T(8,128)S(1)} %fusion.57, s32[5120]{0:T(1024)S(1)} %reshape.2418), kind=kCustom, calls=%fused_computation.7.clone | custom fusion | bytes 102400 | tf_op jit(solution)/shard_map/jit(take_along_axis)/gather | solution.py:169
  472.8 5.9 collective-permute-start.3
  479.6 42.8 %gather_fusion.13 = f32[5120]{0:T(1024)S(1)} fusion(f32[5,16,64]{2,1,0:T(8,128)S(1)} %reshape.2073, s32[5120]{0:T(1024)S(1)} %reshape.2403), kind=kCustom, calls=%fused_computation.4.clone | custom fusion | bytes 102400 | tf_op jit(solution)/shard_map/jit(take_along_axis)/gather | solution.py:169
  525.9 64.7 %gather_fusion.14 = f32[5120]{0:T(1024)} fusion(f32[5,16,64]{2,1,0:T(8,128)S(1)} %subtract_multiply_fusion.1, s32[5120]{0:T(1024)S(1)} %reshape.2408), kind=kCustom, calls=%fused_computation.5.clone | custom fusion | bytes 102400 | tf_op jit(solution)/shard_map/jit(take_along_axis)/gather | solution.py:169
  596.3 6.8 all-to-all-start.3
  606.8 4.4 all-to-all-done.3
  617.0 2.4 scatter_fusion.5
  619.4 2.6 scatter_fusion.6
  622.0 3.9 scatter_fusion.7
  625.9 2.1 slice.641
  628.0 2.1 copy.528
  630.1 2.2 fusion.31
  636.2 2.5 fusion.5
  645.1 2.5 gather_fusion.8
  647.6 2.4 gather_fusion.7
  651.5 2.1 fusion.129
  656.2 2.0 collective-permute-start.4
  660.3 2.0 gather_fusion.6
  663.2 3.5 all-to-all-start.4
  667.1 42.8 %gather_fusion.19 = f32[5120]{0:T(1024)S(1)} fusion(f32[5,16,64]{2,1,0:T(8,128)S(1)} %reshape.2086, s32[5120]{0:T(1024)S(1)} %reshape.2413), kind=kCustom, calls=%fused_computation.10.clone | custom fusion | bytes 102400 | tf_op jit(solution)/shard_map/jit(take_along_axis)/gather | solution.py:169
  710.6 42.8 %gather_fusion.20 = f32[5120]{0:T(1024)S(1)} fusion(f32[5,16,64]{2,1,0:T(8,128)S(1)} %fusion.54, s32[5120]{0:T(1024)S(1)} %reshape.2418), kind=kCustom, calls=%fused_computation.11.clone | custom fusion | bytes 102400 | tf_op jit(solution)/shard_map/jit(take_along_axis)/gather | solution.py:169
  753.6 5.7 collective-permute-start.5
  759.5 42.8 %gather_fusion.17 = f32[5120]{0:T(1024)S(1)} fusion(f32[5,16,64]{2,1,0:T(8,128)S(1)} %reshape.2083, s32[5120]{0:T(1024)S(1)} %reshape.2403), kind=kCustom, calls=%fused_computation.8.clone | custom fusion | bytes 102400 | tf_op jit(solution)/shard_map/jit(take_along_axis)/gather | solution.py:169
  803.0 42.8 %gather_fusion.18 = f32[5120]{0:T(1024)S(1)} fusion(f32[5,16,64]{2,1,0:T(8,128)S(1)} %subtract_multiply_fusion, s32[5120]{0:T(1024)S(1)} %reshape.2408), kind=kCustom, calls=%fused_computation.9.clone | custom fusion | bytes 102400 | tf_op jit(solution)/shard_map/jit(take_along_axis)/gather | solution.py:169
  846.6 6.9 all-to-all-start.5
  853.8 7.7 all-to-all-done.5
  (692 shorter events, 153.5 us)
Async XLA Ops:
  6.2 43.1 %collective-permute-start = (f32[5,1024]{1,0:T(8,128)}, f32[5,1024]{1,0:T(8,128)}, u32[]{:S(2)}, u32[]{:S(2)}) collective-permute-start(f32[5,1024]{1,0:T(8,128)} %reshape.2065), channel_id=1, source_target_pairs={{0,8},{8,16},{16,24},{24,32},{32,40},{40,48},{48,56},{56,64},{64,7... | collective-permute-start | bytes 61448 | tf_op jit(solution)/shard_map/ppermute | solution.py:23
  10.9 164.1 %all-to-all-start = ((f32[5,8,128]{2,0,1:T(8,128)}), f32[5,8,128]{2,0,1:T(8,128)}, u32[]{:S(2)}, u32[]{:S(2)}) async-start(f32[5,8,128]{2,0,1:T(8,128)} %copy.461), calls=%async_computation | async-start | bytes 65536 | tf_op jit(solution)/shard_map/all_to_all | solution.py:244
  18.5 98.8 %copy-start.22 = (s32[16,64]{1,0:T(8,128)}, s32[16,64]{1,0:T(8,128)S(1)}, u32[]{:S(2)}) copy-start(s32[16,64]{1,0:T(8,128)S(1)} %get-tuple-element.10) | copy-start | bytes 12292
  18.5 141.8 %copy-start.62 = (s32[16,64]{1,0:T(8,128)}, s32[16,64]{1,0:T(8,128)S(1)}, u32[]{:S(2)}) copy-start(s32[16,64]{1,0:T(8,128)S(1)} %get-tuple-element.11) | copy-start | bytes 12292
  18.5 203.6 %copy-start.25 = (s32[16,64]{1,0:T(8,128)}, s32[16,64]{1,0:T(8,128)S(1)}, u32[]{:S(2)}) copy-start(s32[16,64]{1,0:T(8,128)S(1)} %get-tuple-element.9) | copy-start | bytes 12292
  18.5 270.3 %copy-start.59 = (s32[16,64]{1,0:T(8,128)}, s32[16,64]{1,0:T(8,128)S(1)}, u32[]{:S(2)}) copy-start(s32[16,64]{1,0:T(8,128)S(1)} %get-tuple-element.8) | copy-start | bytes 12292
  18.5 98.8 %copy-start.34 = (s32[16,64]{1,0:T(8,128)}, s32[16,64]{1,0:T(8,128)S(1)}, u32[]{:S(2)}) copy-start(s32[16,64]{1,0:T(8,128)S(1)} %get-tuple-element.158) | copy-start | bytes 12292
  18.5 141.7 %copy-start.78 = (s32[16,64]{1,0:T(8,128)}, s32[16,64]{1,0:T(8,128)S(1)}, u32[]{:S(2)}) copy-start(s32[16,64]{1,0:T(8,128)S(1)} %get-tuple-element.157) | copy-start | bytes 12292
  19.2 202.8 %copy-start.37 = (s32[16,64]{1,0:T(8,128)}, s32[16,64]{1,0:T(8,128)S(1)}, u32[]{:S(2)}) copy-start(s32[16,64]{1,0:T(8,128)S(1)} %get-tuple-element.159) | copy-start | bytes 12292
  19.9 202.2 %copy-start.89 = (pred[16,64]{1,0:T(8,128)(4,1)}, pred[16,64]{1,0:T(8,128)(4,1)S(1)}, u32[]{:S(2)}) copy-start(pred[16,64]{1,0:T(8,128)(4,1)S(1)} %get-tuple-element.163) | copy-start | bytes 3076
  50.1 65.4 %copy-start.93 = (pred[16,64]{1,0:T(8,128)(4,1)S(1)}, pred[16,64]{1,0:T(8,128)(4,1)}, u32[]{:S(2)}) copy-start(pred[16,64]{1,0:T(8,128)(4,1)} %copy-done.92) | copy-start | bytes 3076
  50.1 65.5 %copy-start.31 = (f32[32,5,64]{2,0,1:T(8,128)S(1)}, f32[32,5,64]{2,0,1:T(8,128)}, u32[]{:S(2)}) copy-start(f32[32,5,64]{2,0,1:T(8,128)} %copy-done.30) | copy-start | bytes 122884
  50.1 65.5 %copy-start.123 = (f32[3,16]{1,0:T(4,128)S(1)}, f32[3,16]{1,0:T(4,128)}, u32[]{:S(2)}) copy-start(f32[3,16]{1,0:T(4,128)} %copy-done.122) | copy-start | bytes 580
  50.2 65.5 %copy-start.99 = (f32[16]{0:T(128)S(1)}, f32[16]{0:T(128)}, u32[]{:S(2)}) copy-start(f32[16]{0:T(128)} %fusion.109) | copy-start | bytes 196
  50.2 67.0 %copy-start.162 = (f32[16]{0:T(128)S(1)}, f32[16]{0:T(128)}, u32[]{:S(2)}) copy-start(f32[16]{0:T(128)} %get-tuple-element.69) | copy-start | bytes 196
  50.2 67.1 %copy-start.159 = (f32[16]{0:T(128)S(1)}, f32[16]{0:T(128)}, u32[]{:S(2)}) copy-start(f32[16]{0:T(128)} %get-tuple-element.144) | copy-start | bytes 196
  161.0 140.1 %collective-permute-start.1 = (f32[5,1024]{1,0:T(8,128)}, f32[5,1024]{1,0:T(8,128)}, u32[]{:S(2)}, u32[]{:S(2)}) collective-permute-start(f32[5,1024]{1,0:T(8,128)} %reshape.2067), channel_id=1, source_target_pairs={{8,0},{16,8},{24,16},{32,24},{40,32},{48,40},{56,48},{64,56},{72,6... | collective-permute-start | bytes 61448 | tf_op jit(solution)/shard_map/ppermute | solution.py:23
  175.9 43.7 %copy-start.96 = (f32[16]{0:T(128)S(1)}, f32[16]{0:T(128)}, u32[]{:S(2)}) copy-start(f32[16]{0:T(128)} %get-tuple-element.153) | copy-start | bytes 196
  175.9 46.2 %copy-start.58 = (f32[16,5,64]{2,1,0:T(8,128)S(1)}, f32[16,5,64]{2,1,0:T(8,128)}, u32[]{:S(2)}) copy-start(f32[16,5,64]{2,1,0:T(8,128)} %copy-done.57) | copy-start | bytes 61444
  222.8 66.0 %copy-start.75 = (s32[16,64]{1,0:T(8,128)S(1)}, s32[16,64]{1,0:T(8,128)}, u32[]{:S(2)}) copy-start(s32[16,64]{1,0:T(8,128)} %copy-done.74) | copy-start | bytes 12292
  293.0 15.5 %all-to-all-start.1 = ((f32[5,8,128]{2,0,1:T(8,128)}), f32[5,8,128]{2,0,1:T(8,128)}, u32[]{:S(2)}, u32[]{:S(2)}) async-start(f32[5,8,128]{2,0,1:T(8,128)} %copy.464), calls=%async_computation.1 | async-start | bytes 65536 | tf_op jit(solution)/shard_map/all_to_all | solution.py:261
  356.4 27.5 %collective-permute-start.2 = (f32[5,1024]{1,0:T(8,128)}, f32[5,1024]{1,0:T(8,128)}, u32[]{:S(2)}, u32[]{:S(2)}) collective-permute-start(f32[5,1024]{1,0:T(8,128)} %reshape.2075), channel_id=1, source_target_pairs={{0,8},{8,16},{16,24},{24,32},{32,40},{40,48},{48,56},{56,64},{64,7... | collective-permute-start | bytes 61448 | tf_op jit(solution)/shard_map/ppermute | solution.py:23
  377.0 101.7 %all-to-all-start.2 = ((f32[5,8,128]{2,0,1:T(8,128)}), f32[5,8,128]{2,0,1:T(8,128)}, u32[]{:S(2)}, u32[]{:S(2)}) async-start(f32[5,8,128]{2,0,1:T(8,128)} %copy.482), calls=%async_computation.2 | async-start | bytes 65536 | tf_op jit(solution)/shard_map/all_to_all | solution.py:244
  384.8 43.2 %copy-start.165 = (f32[16]{0:T(128)S(1)}, f32[16]{0:T(128)}, u32[]{:S(2)}) copy-start(f32[16]{0:T(128)} %get-tuple-element.70) | copy-start | bytes 196
  384.8 43.3 %copy-start.163 = (f32[16]{0:T(128)S(1)}, f32[16]{0:T(128)}, u32[]{:S(2)}) copy-start(f32[16]{0:T(128)} %get-tuple-element.69) | copy-start | bytes 196
  384.8 43.5 %copy-start.160 = (f32[16]{0:T(128)S(1)}, f32[16]{0:T(128)}, u32[]{:S(2)}) copy-start(f32[16]{0:T(128)} %get-tuple-element.144) | copy-start | bytes 196
  472.8 131.0 %collective-permute-start.3 = (f32[5,1024]{1,0:T(8,128)}, f32[5,1024]{1,0:T(8,128)}, u32[]{:S(2)}, u32[]{:S(2)}) collective-permute-start(f32[5,1024]{1,0:T(8,128)} %reshape.2077), channel_id=1, source_target_pairs={{8,0},{16,8},{24,16},{32,24},{40,32},{48,40},{56,48},{64,56},{72,6... | collective-permute-start | bytes 61448 | tf_op jit(solution)/shard_map/ppermute | solution.py:23
  479.6 43.8 %copy-start.97 = (f32[16]{0:T(128)S(1)}, f32[16]{0:T(128)}, u32[]{:S(2)}) copy-start(f32[16]{0:T(128)} %get-tuple-element.153) | copy-start | bytes 196
  479.6 43.9 %copy-start.157 = (f32[16]{0:T(128)S(1)}, f32[16]{0:T(128)}, u32[]{:S(2)}) copy-start(f32[16]{0:T(128)} %get-tuple-element.74) | copy-start | bytes 196
  479.6 44.6 %copy-start.155 = (f32[16]{0:T(128)S(1)}, f32[16]{0:T(128)}, u32[]{:S(2)}) copy-start(f32[16]{0:T(128)} %get-tuple-element.73) | copy-start | bytes 196
  479.6 45.4 %copy-start.153 = (f32[16]{0:T(128)S(1)}, f32[16]{0:T(128)}, u32[]{:S(2)}) copy-start(f32[16]{0:T(128)} %get-tuple-element.72) | copy-start | bytes 196
  479.6 46.2 %copy-start.150 = (f32[16]{0:T(128)S(1)}, f32[16]{0:T(128)}, u32[]{:S(2)}) copy-start(f32[16]{0:T(128)} %reshape.2099) | copy-start | bytes 196
  525.9 66.2 %copy-start.60 = (s32[16,64]{1,0:T(8,128)S(1)}, s32[16,64]{1,0:T(8,128)}, u32[]{:S(2)}) copy-start(s32[16,64]{1,0:T(8,128)} %copy-done.59) | copy-start | bytes 12292
  525.9 66.2 %copy-start.76 = (s32[16,64]{1,0:T(8,128)S(1)}, s32[16,64]{1,0:T(8,128)}, u32[]{:S(2)}) copy-start(s32[16,64]{1,0:T(8,128)} %copy-done.74) | copy-start | bytes 12292
  596.3 14.9 %all-to-all-start.3 = ((f32[5,8,128]{2,0,1:T(8,128)}), f32[5,8,128]{2,0,1:T(8,128)}, u32[]{:S(2)}, u32[]{:S(2)}) async-start(f32[5,8,128]{2,0,1:T(8,128)} %copy.484), calls=%async_computation.3 | async-start | bytes 65536 | tf_op jit(solution)/shard_map/all_to_all | solution.py:261
  656.2 10.8 %collective-permute-start.4 = (f32[5,1024]{1,0:T(8,128)S(1)}, f32[5,1024]{1,0:T(8,128)S(1)}, u32[]{:S(2)}, u32[]{:S(2)}) collective-permute-start(f32[5,1024]{1,0:T(8,128)S(1)} %reshape.2085), channel_id=1, source_target_pairs={{0,8},{8,16},{16,24},{24,32},{32,40},{40,48},{48,56},{56,64},{64,7... | collective-permute-start | bytes 61448 | tf_op jit(solution)/shard_map/ppermute | solution.py:23
  660.3 49.6 %copy-start.49 = (f32[5,192,64]{1,2,0:T(8,128)}, f32[5,192,64]{1,2,0:T(8,128)S(1)}, u32[]{:S(2)}) copy-start(f32[5,192,64]{1,2,0:T(8,128)S(1)} %get-tuple-element.75) | copy-start | bytes 737284
  660.3 49.6 %copy-start.51 = (f32[5,192,64]{1,2,0:T(8,128)}, f32[5,192,64]{1,2,0:T(8,128)S(1)}, u32[]{:S(2)}) copy-start(f32[5,192,64]{1,2,0:T(8,128)S(1)} %get-tuple-element.76) | copy-start | bytes 737284
  663.2 96.1 %all-to-all-start.4 = ((f32[5,8,128]{2,0,1:T(8,128)}), f32[5,8,128]{2,0,1:T(8,128)S(1)}, u32[]{:S(2)}, u32[]{:S(2)}) async-start(f32[5,8,128]{2,0,1:T(8,128)} %copy.501), calls=%async_computation.4 | async-start | bytes 65536 | tf_op jit(solution)/shard_map/all_to_all | solution.py:244
  667.0 43.2 %copy-start.166 = (f32[16]{0:T(128)S(1)}, f32[16]{0:T(128)}, u32[]{:S(2)}) copy-start(f32[16]{0:T(128)} %get-tuple-element.70) | copy-start | bytes 196
  667.1 43.3 %copy-start.164 = (f32[16]{0:T(128)S(1)}, f32[16]{0:T(128)}, u32[]{:S(2)}) copy-start(f32[16]{0:T(128)} %get-tuple-element.69) | copy-start | bytes 196
  667.1 43.4 %copy-start.161 = (f32[16]{0:T(128)S(1)}, f32[16]{0:T(128)}, u32[]{:S(2)}) copy-start(f32[16]{0:T(128)} %get-tuple-element.144) | copy-start | bytes 196
  753.6 100.0 %collective-permute-start.5 = (f32[5,1024]{1,0:T(8,128)S(1)}, f32[5,1024]{1,0:T(8,128)S(1)}, u32[]{:S(2)}, u32[]{:S(2)}) collective-permute-start(f32[5,1024]{1,0:T(8,128)S(1)} %reshape.2087), channel_id=1, source_target_pairs={{8,0},{16,8},{24,16},{32,24},{40,32},{48,40},{56,48},{64,56},{72,6... | collective-permute-start | bytes 61448 | tf_op jit(solution)/shard_map/ppermute | solution.py:23
  759.4 43.2 %copy-start.156 = (f32[16]{0:T(128)S(1)}, f32[16]{0:T(128)}, u32[]{:S(2)}) copy-start(f32[16]{0:T(128)} %get-tuple-element.73) | copy-start | bytes 196
  759.5 43.3 %copy-start.154 = (f32[16]{0:T(128)S(1)}, f32[16]{0:T(128)}, u32[]{:S(2)}) copy-start(f32[16]{0:T(128)} %get-tuple-element.72) | copy-start | bytes 196
  759.5 43.4 %copy-start.151 = (f32[16]{0:T(128)S(1)}, f32[16]{0:T(128)}, u32[]{:S(2)}) copy-start(f32[16]{0:T(128)} %reshape.2099) | copy-start | bytes 196
  803.0 50.7 %copy-start.152 = (f32[16]{0:T(128)S(1)}, f32[16]{0:T(128)}, u32[]{:S(2)}) copy-start(f32[16]{0:T(128)} %get-tuple-element.143) | copy-start | bytes 196
  846.6 14.9 %all-to-all-start.5 = ((f32[5,8,128]{2,0,1:T(8,128)}), f32[5,8,128]{2,0,1:T(8,128)S(1)}, u32[]{:S(2)}, u32[]{:S(2)}) async-start(f32[5,8,128]{2,0,1:T(8,128)} %copy.503), calls=%async_computation.5 | async-start | bytes 65536 | tf_op jit(solution)/shard_map/all_to_all | solution.py:261
  (153 other events, 2350.4 us)
where the time goes:
time: 883 us; the launch traced here: 871 us
  local copies, waits for them, and re-layouts  691 us (78%)
  starting transfers between devices  67.2 us (8%)
  other arithmetic  63.5 us (7%)
  matrix products  30 us (3%)
  waiting for transfers between devices  16.6 us (2%)
    gather x28, local copies, waits for them, and re-layouts, orient(): jnp.take_along_axis(values, jnp.broadcast_to(gather_index[None], values.s...  585 us
    ppermute x6, starting transfers between devices, from_behind(): return lax.ppermute(block, axis, route)  31.5 us
    all_to_all x3, starting transfers between devices, rhs(): lax.all_to_all(returned, 'tile', split_axis=1, concat_axis=1, tiled=True)  21.1 us
  transfers between devices with their start and end apart: 12, of which 3 were waited for; matrix products, arithmetic and copies ran while one was open for 77% of the time, Pallas kernels for 0%

commit v1 on v0

v1 whole, which is shorter than its diff:
```python
import jax
import jax.numpy as jnp
import numpy as np
from jax import lax
from jax.experimental import pallas as pl
from jax.experimental.pallas import tpu as pltpu
from jax.sharding import PartitionSpec as P


time_step = 0.002
inner_nodes = [
    -0.8717401485096066,
    -0.5917001814331423,
    -0.20929921790247888,
    0.20929921790247888,
    0.5917001814331423,
    0.8717401485096066,
]
f32, bf16, i32 = jnp.float32, jnp.bfloat16, jnp.int32

PERM, INV, PICK, SPREAD, INDEX_ROWS = 0, 128, 256, 288, 416
CHILD, SEND_Z, RECV_Z, RECV_LIVE, CURVE_LIVE = 0, 8, 16, 24, 32


def legendre_seven(abscissa):
    before = abscissa * 0.0 + 1.0
    current = abscissa + 0.0
    for order in range(1, 7):
        before, current = (
            current,
            ((2 * order + 1) * abscissa * current - order * before) / (order + 1),
        )
    return current


def split_np(array):
    array = np.asarray(array, np.float32).astype(np.float64)
    high = array.astype(bf16).astype(np.float64)
    low = (array - high).astype(bf16).astype(np.float64)
    return high, low


def tables():
    degree = 7
    points = np.array([-1.0] + inner_nodes + [1.0])
    values = legendre_seven(points)
    weights = 2.0 / (degree * (degree + 1) * values**2)
    deriv = np.zeros((8, 8))
    for i in range(8):
        for m in range(8):
            if i != m:
                deriv[i, m] = values[i] / (values[m] * (points[i] - points[m]))
    deriv[0, 0] = -degree * (degree + 1) / 4.0
    deriv[7, 7] = degree * (degree + 1) / 4.0
    weak = -deriv
    weak[0, 0] -= 28.0
    weak[7, 7] += 28.0
    halves, projections = [], []
    for side in range(2):
        targets = (points + 2.0 * side - 1.0) / 2.0
        interp = np.ones((8, 8))
        for m in range(8):
            for other in range(8):
                if other != m:
                    interp[:, m] *= (targets - points[other]) / (points[m] - points[other])
        halves.append(interp)
        projections.append(0.5 * (interp.T * weights[None, :]) / weights[:, None])

    def child_weights(parts):
        columns = [
            np.kron(np.eye(2), np.kron(parts[a], parts[b]).T) for a in range(2) for b in range(2)
        ]
        high, low = split_np(np.concatenate(columns, axis=1))
        return np.concatenate([high, high, low], axis=0)

    def tile_weights(matrix):
        high, low = split_np(matrix.T)
        return np.block([[high, low], [high, np.zeros_like(high)]])

    along_y = np.kron(np.eye(2), np.kron(weak, np.eye(8)))
    along_z = np.kron(np.eye(16), weak)
    derivs = np.concatenate([tile_weights(along_y), tile_weights(along_z)], axis=1)
    mats = np.concatenate([child_weights(halves), child_weights(projections), derivs], axis=0)
    coefs = np.zeros((32, 128))
    for a in range(4):
        for b in range(4):
            coefs[a * 4 + b, :64] = weak[2 * a, 2 * b]
            coefs[a * 4 + b, 64:] = weak[2 * a + 1, 2 * b + 1]
            coefs[16 + a * 4 + b, :64] = weak[2 * a, 2 * b + 1]
            coefs[16 + a * 4 + b, 64:] = weak[2 * a + 1, 2 * b]

    perm = np.zeros((8, 64), np.int64)
    for code in range(8):
        for s in range(8):
            for t in range(8):
                a, c = (t, s) if code & 4 else (s, t)
                a = 7 - a if code & 1 else a
                c = 7 - c if code & 2 else c
                perm[code, 8 * s + t] = 8 * a + c
    inverse = np.argsort(perm, axis=1)
    lane = np.arange(128)
    rows = []
    for table in (perm, inverse):
        for half in range(2):
            for code in range(8):
                rows.append(table[code][lane % 64] + 64 * half)
    slot_lane = lane % 64
    i, rest = slot_lane // 8, slot_lane % 8
    for end in (7, 0):
        rows.append(64 * (i % 2) + 8 * end + rest)
        rows.append(64 * (i % 2) + 8 * rest + end)
    for kind in range(2):
        for half in range(2):
            for tile in range(4):
                first = 2 * tile + lane // 64
                second = lane % 8 if kind == 0 else (lane // 8) % 8
                rows.append(8 * first + second + 64 * half)
    index = np.repeat(np.stack(rows), 8, axis=0)
    return (
        jnp.asarray(index, i32),
        jnp.asarray(mats, f32).astype(bf16),
        jnp.asarray(coefs, f32),
    )


def take(values, index):
    return jnp.take_along_axis(values, index, axis=1, mode="promise_in_bounds")


def lanes():
    return lax.broadcasted_iota(i32, (8, 128), 1)


def split(values):
    high = values.astype(bf16)
    return high, (values - high.astype(f32)).astype(bf16)


def row(ref, start):
    return ref[pl.ds(pl.multiple_of(start, 8), 8), :]


def child_map(pieces, mats_ref, start, codes):
    high, low = split(jnp.concatenate(pieces, axis=0))
    mapped = jnp.dot(
        jnp.concatenate([high, low, high], axis=1),
        mats_ref[start : start + 384, :],
        preferred_element_type=f32,
    )
    out = []
    for f, piece in enumerate(pieces):
        total = jnp.where(codes == 4, piece, 0.0)
        for c in range(4):
            total = jnp.where(codes == c, mapped[8 * f : 8 * f + 8, 128 * c : 128 * c + 128], total)
        out.append(total)
    return out


def neighbour_part(q, sign, is_z, scale):
    normal = jnp.where(is_z, q[3], q[2]) * sign
    push = q[4] * sign
    return [
        (normal - q[0]) * scale,
        q[1] * -scale,
        (jnp.where(is_z, 0.0, push) - q[2]) * scale,
        (jnp.where(is_z, push, 0.0) - q[3]) * scale,
        (normal - q[4]) * scale,
    ]


def pack_curve(u_ref, slots, masks_ref, index_ref, tmp, left_ref, right_ref):
    low = lanes() < 64
    for side, out_ref, sign in ((0, left_ref, 1.0), (1, right_ref, -1.0)):
        for k in range(8):
            picked = []
            for s in (16 * side + k, 16 * side + k + 8):
                trace = row(u_ref, slots[s] + 768 * side)
                picked.append(take(trace, row(index_ref, slots[64 + s] + INV + 64 * side)))
            tmp[64 * side + 8 * k : 64 * side + 8 * k + 8, :] = jnp.where(low, *picked)
        q = [tmp[pl.ds(64 * side + f, 8, stride=8), :] for f in range(5)]
        scale = masks_ref[CURVE_LIVE + 8 * side : CURVE_LIVE + 8 * side + 8, :] * 14.0
        parts = [
            (sign * q[1] - q[0]) * scale,
            (sign * q[4] - q[1]) * scale,
            q[2] * -scale,
            q[3] * -scale,
            (sign * q[1] - q[4]) * scale,
        ]
        for f in range(5):
            out_ref[pl.ds(f, 8, stride=8), :] = parts[f]


def pack_tile(u_ref, slots, masks_ref, index_ref, mats_ref, tmp, own_ref, tile_ref):
    low = lanes() < 64
    quarter = (lanes() % 64) // 16
    for side in range(2):
        for p in range(8):
            picked = []
            for k in range(2):
                s = 32 + 16 * side + 2 * p + k
                index = row(index_ref, slots[128 + s] * 8 + PICK + 16 * side)
                trace = take(row(u_ref, slots[s]), index)
                for a in range(1, 4):
                    other = take(row(u_ref, slots[s] + 256 * a), index)
                    trace = jnp.where(quarter == a, other, trace)
                picked.append(trace)
            pair = jnp.where(low, *picked)
            if side == 1:
                s = 48 + 2 * p
                pair = jnp.where(
                    low,
                    take(pair, row(index_ref, slots[64 + s] + INV)),
                    take(pair, row(index_ref, slots[65 + s] + INV + 64)),
                )
            tmp[64 * side + 8 * p : 64 * side + 8 * p + 8, :] = pair
    q = [tmp[pl.ds(f, 8, stride=8), :] for f in range(5)]
    q = child_map(q, mats_ref, 0, masks_ref[CHILD : CHILD + 8, :])
    is_z = masks_ref[SEND_Z : SEND_Z + 8, :] > 0.0
    for f, part in enumerate(neighbour_part(q, -1.0, is_z, 14.0)):
        tile_ref[pl.ds(f, 8, stride=16), :] = part
        own_ref[pl.ds(f, 8, stride=8), :] = part
    q = [tmp[pl.ds(64 + f, 8, stride=8), :] for f in range(5)]
    is_z = masks_ref[RECV_Z : RECV_Z + 8, :] > 0.0
    scale = masks_ref[RECV_LIVE : RECV_LIVE + 8, :] * 14.0
    for f, part in enumerate(neighbour_part(q, 1.0, is_z, scale)):
        tile_ref[pl.ds(8 + f, 8, stride=16), :] = part


def spread(w_ref, pair, slots, s, half, end, index_ref):
    kind = slots[128 + s]
    lane = lanes()
    position = jnp.where(kind == 0, (lane // 8) % 8, lane % 8)
    at_face = position == end
    for a in range(4):
        moved = take(pair, row(index_ref, kind * 64 + SPREAD + 32 * half + 8 * a))
        block = pl.ds(pl.multiple_of(slots[s] + 256 * a, 8), 8)
        w_ref[block, :] = w_ref[block, :] - jnp.where(at_face, moved, 0.0)


def unpack(w_ref, slots, masks_ref, index_ref, mats_ref, tmp, from_left, from_right, tile_ref, own_ref):
    low = lanes() < 64
    q = [
        tile_ref[pl.ds(8 + f, 8, stride=16), :] - own_ref[pl.ds(f, 8, stride=8), :]
        for f in range(5)
    ]
    q = child_map(q, mats_ref, 384, masks_ref[CHILD : CHILD + 8, :])
    for f in range(5):
        tmp[pl.ds(f, 8, stride=8), :] = q[f]
    for side, in_ref in ((0, from_left), (1, from_right)):
        for k in range(8):
            pair = in_ref[8 * k : 8 * k + 8, :]
            turned = pltpu.roll(pair, 64, 1)
            for s, value in ((k, (pair, turned)[side]), (k + 8, (turned, pair)[side])):
                block = pl.ds(pl.multiple_of(slots[16 * side + s] + 768 * side, 8), 8)
                kept = jnp.where(low, value, 0.0) if side == 0 else jnp.where(low, 0.0, value)
                w_ref[block, :] = w_ref[block, :] - kept
    for p in range(8):
        s = 48 + 2 * p
        pair = tile_ref[16 * p : 16 * p + 8, :]
        pair = jnp.where(
            low,
            take(pair, row(index_ref, slots[64 + s] + PERM)),
            take(pair, row(index_ref, slots[65 + s] + PERM + 64)),
        )
        for k in range(2):
            spread(w_ref, pair, slots, s + k, k, 0, index_ref)
    for p in range(8):
        pair = tmp[8 * p : 8 * p + 8, :]
        for k in range(2):
            spread(w_ref, pair, slots, 32 + 2 * p + k, k, 7, index_ref)


def inside(u_ref, faces_ref, mats_ref, coefs_ref, w_ref):
    fields = [[u_ref[pl.ds(256 * a + f, 32, stride=8), :] for a in range(4)] for f in range(5)]
    dens, vx, vy, vz, pres = fields

    def along(vel, start):
        stacked = [values[a] for values in (vel, pres) for a in range(4)]
        high, low = split(jnp.concatenate(stacked, axis=0))
        both = jnp.dot(
            jnp.concatenate([high, low], axis=1),
            mats_ref[768:1024, start : start + 256],
            preferred_element_type=f32,
        )
        both = both[:, :128] + both[:, 128:]
        return [both[32 * n : 32 * n + 32] for n in range(8)]

    grad_y = along(vy, 0)
    grad_z = along(vz, 256)
    grad_x = []
    for values in (vx, pres):
        plain = values
        turned = [pltpu.roll(t, 64, 1) for t in plain]
        for a in range(4):
            total = None
            for b in range(4):
                n = 4 * a + b
                term = plain[b] * coefs_ref[n : n + 1, :] + turned[b] * coefs_ref[16 + n : 17 + n, :]
                total = term if total is None else total + term
            grad_x.append(total)
    face = [faces_ref[32 * n : 32 * n + 32, :] for n in range(11)]
    ay, az, ayz, ax0, ux0, ax3, ux3, uy0, uy7, uz0, uz7 = face
    for a in range(4):
        d, x, y, z, p = (values[a] for values in fields)
        asum = ayz
        inward = -(ay * y + az * z)
        if a == 0:
            asum = asum + ax0
            inward = inward - ax0 * x
        elif a == 3:
            asum = asum + ax3
            inward = inward + ax3 * x
        diverge = grad_x[a] + grad_y[a] + grad_z[a] - inward
        out = [diverge - asum * d, grad_x[4 + a] - ayz * x, None, None, diverge - asum * p]
        if a == 0:
            out[1] = out[1] + ux0 * (p - x)
        elif a == 3:
            out[1] = out[1] - ux3 * (p + x)
        out[2] = grad_y[4 + a] + uy0 * (p - y) - uy7 * (p + y) - (asum - ay) * y
        out[3] = grad_z[4 + a] + uz0 * (p - z) - uz7 * (p + z) - (asum - az) * z
        for f in range(5):
            w_ref[pl.ds(256 * a + f, 32, stride=8), :] = out[f]


def first_kernel(
    state_hbm, levels_hbm, send_faces_hbm, send_counts_hbm, recv_faces_hbm, recv_orients_hbm,
    recv_counts_hbm, curve_faces_hbm, curve_orients_hbm, curve_counts_hbm, index_hbm, mats_hbm,
    u_ref, left_ref, right_ref, own_ref, tile_hbm, slots, masks_ref,
    levels, send_faces, send_counts, recv_faces, recv_orients, recv_counts, curve_faces,
    curve_orients, curve_counts, state_ref, index_ref, mats_ref, tmp, tile_ref, sems,
):
    numbers = [
        pltpu.make_async_copy(source, target, sems.at[n])
        for n, (source, target) in enumerate(
            (
                (curve_faces_hbm, curve_faces),
                (curve_orients_hbm, curve_orients),
                (curve_counts_hbm, curve_counts),
                (send_faces_hbm, send_faces),
                (send_counts_hbm, send_counts),
                (recv_faces_hbm, recv_faces),
                (recv_orients_hbm, recv_orients),
                (recv_counts_hbm, recv_counts),
                (levels_hbm, levels),
            )
        )
    ]
    arrays = [
        pltpu.make_async_copy(source, target, sems.at[9 + n])
        for n, (source, target) in enumerate(
            (
                (state_hbm, state_ref),
                (index_hbm, index_ref),
                (mats_hbm.at[pl.ds(0, 384), :], mats_ref),
            )
        )
    ]
    for copy in numbers + arrays:
        copy.start()
    for copy in numbers:
        copy.wait()
    low = lax.broadcasted_iota(i32, (1, 128), 1) < 64

    def halves(a, b):
        return jnp.where(low, a, b)

    for side in range(2):
        live = []
        for k in range(16):
            s = 16 * side + k
            is_live = k < curve_counts[side]
            element = (curve_faces[side, k] * 10923) >> 16
            slots[s] = element * 8
            slots[64 + s] = curve_orients[side, k] * 8
            slots[128 + s] = 0
            slots[192 + s] = jnp.where(is_live, 32 * side + element, 192)
            live.append(jnp.where(is_live, 1.0, 0.0))
        for k in range(8):
            at = CURVE_LIVE + 8 * side + k
            masks_ref[at : at + 1, :] = halves(live[k], live[k + 8])
    for p in range(8):
        child, kinds, recv_kinds, recv_live = [], [], [], []
        for k in range(2):
            s = 32 + 2 * p + k
            number = send_faces[k, p]
            is_live = k < send_counts[p]
            element = (number * 2185) >> 16
            rest = number - 30 * element
            is_z = rest >= 25
            slots[s] = element * 8
            slots[64 + s] = 0
            slots[128 + s] = jnp.where(is_z, 1, 0)
            slots[192 + s] = jnp.where(is_live, jnp.where(is_z, 160, 96) + element, 192)
            child.append(jnp.where(is_live, jnp.where(is_z, rest - 25, rest - 15), -1))
            kinds.append(jnp.where(is_z, 1.0, 0.0))
            s = 48 + 2 * p + k
            number = recv_faces[k, p]
            is_live = k < recv_counts[p]
            element = (number * 10923) >> 16
            is_z = number - 6 * element == 4
            slots[s] = element * 8
            slots[64 + s] = recv_orients[k, p] * 8
            slots[128 + s] = jnp.where(is_z, 1, 0)
            slots[192 + s] = jnp.where(is_live, jnp.where(is_z, 128, 64) + element, 192)
            recv_kinds.append(jnp.where(is_z, 1.0, 0.0))
            recv_live.append(jnp.where(is_live, 1.0, 0.0))
        masks_ref[CHILD + p : CHILD + p + 1, :] = halves(*child).astype(f32)
        masks_ref[SEND_Z + p : SEND_Z + p + 1, :] = halves(*kinds)
        masks_ref[RECV_Z + p : RECV_Z + p + 1, :] = halves(*recv_kinds)
        masks_ref[RECV_LIVE + p : RECV_LIVE + p + 1, :] = halves(*recv_live)
    for e in range(32):
        slots[256 + e] = 1 << levels[e]
    for copy in arrays:
        copy.wait()
    for f in range(5):
        for a in range(4):
            u_ref[pl.ds(256 * a + f, 32, stride=8), :] = state_ref[f, :, 128 * a : 128 * a + 128]
    pack_tile(u_ref, slots, masks_ref, index_ref, mats_ref, tmp, own_ref, tile_ref)
    send = pltpu.make_async_copy(tile_ref, tile_hbm, sems.at[12])
    send.start()
    pack_curve(u_ref, slots, masks_ref, index_ref, tmp, left_ref, right_ref)
    send.wait()


def faces_kernel(slots, faces_ref, scale_ref, listed):
    listed[...] = jnp.zeros_like(listed)
    for s in range(64):
        listed[pl.ds(slots[192 + s], 1), :] = jnp.ones((1, 128), f32)
    for e in range(32):
        scale_ref[8 * e : 8 * e + 8, :] = (
            jnp.full((8, 128), slots[256 + e], i32).astype(f32) * time_step
        )
    lane = lax.broadcasted_iota(i32, (32, 128), 1)
    on = [listed[32 * f : 32 * f + 32, :] for f in range(6)]
    where_0 = [lane < 64, (lane // 8) % 8 == 0, lane % 8 == 0]
    where_7 = [lane >= 64, (lane // 8) % 8 == 7, lane % 8 == 7]

    def keep(test, values):
        return jnp.where(test, values, 0.0)

    ay = keep(where_0[1], 14.0 * on[2])
    az = keep(where_0[2], 14.0 * on[4])
    values = [
        ay,
        az,
        ay + az,
        keep(where_0[0], 14.0 * on[0]),
        keep(where_0[0], 28.0 - 14.0 * on[0]),
        keep(where_7[0], 14.0 * on[1]),
        keep(where_7[0], 28.0 - 14.0 * on[1]),
        keep(where_0[1], 28.0 - 14.0 * on[2]),
        keep(where_7[1], 28.0 - 28.0 * on[3]),
        keep(where_0[2], 28.0 - 14.0 * on[4]),
        keep(where_7[2], 28.0 - 28.0 * on[5]),
    ]
    for n, value in enumerate(values):
        faces_ref[32 * n : 32 * n + 32, :] = value


def next_kernel(
    slots_any, u_ref, from_left, from_right, arrived_ref, sent_ref, masks_ref, faces_ref, scale_ref,
    index_ref, mats_ref, coefs_ref,
    out_ref, left_ref, right_ref, own_ref, tile_hbm, w_ref, tmp, slots, tile_ref, sems,
):
    fetch = pltpu.make_async_copy(slots_any, slots, sems.at[0])
    fetch.start()
    inside(u_ref, faces_ref, mats_ref, coefs_ref, w_ref)
    fetch.wait()
    unpack(
        w_ref, slots, masks_ref, index_ref, mats_ref, tmp, from_left, from_right, arrived_ref, sent_ref
    )
    for a in range(4):
        out_ref[256 * a : 256 * a + 256, :] = w_ref[256 * a : 256 * a + 256, :] * scale_ref[...]
    pack_tile(out_ref, slots, masks_ref, index_ref, mats_ref, tmp, own_ref, tile_ref)
    send = pltpu.make_async_copy(tile_ref, tile_hbm, sems.at[1])
    send.start()
    pack_curve(out_ref, slots, masks_ref, index_ref, tmp, left_ref, right_ref)
    send.wait()


def last_kernel(
    slots_any, u_ref, from_left, from_right, arrived_ref, sent_ref, masks_ref, faces_ref, scale_ref,
    index_ref, mats_ref, coefs_ref, state_ref, first_ref,
    out_ref, w_ref, tmp, slots, sems,
):
    fetch = pltpu.make_async_copy(slots_any, slots, sems.at[0])
    fetch.start()
    inside(u_ref, faces_ref, mats_ref, coefs_ref, w_ref)
    fetch.wait()
    unpack(
        w_ref, slots, masks_ref, index_ref, mats_ref, tmp, from_left, from_right, arrived_ref, sent_ref
    )
    scale = scale_ref[pl.ds(0, 32, stride=8), :] * (1.0 / 6.0)
    for f in range(5):
        for a in range(4):
            at = (pl.ds(256 * a + f, 32, stride=8), slice(None))
            column = slice(128 * a, 128 * a + 128)
            out_ref[f, :, column] = (
                state_ref[f, :, column] + first_ref[at] + 0.5 * u_ref[at] + w_ref[at] * scale
            )


def shards(
    state, levels, send_faces, send_counts, recv_faces, recv_orients, recv_counts,
    curve_faces, curve_orients, curve_counts,
):
    index, mats, coefs = tables()
    vmem = pl.BlockSpec(memory_space=pltpu.VMEM)
    smem = pl.BlockSpec(memory_space=pltpu.SMEM)
    hbm = pl.BlockSpec(memory_space=pltpu.HBM)
    anywhere = pl.BlockSpec(memory_space=pl.ANY)

    def shape(*dims, kind=f32):
        return jax.ShapeDtypeStruct(dims, kind)

    def call(kernel, name, **kwargs):
        return pl.pallas_call(
            kernel,
            name=name,
            compiler_params=pltpu.CompilerParams(vmem_limit_bytes=16 * 1024 * 1024),
            **kwargs,
        )

    payload = [shape(64, 128)] * 3 + [shape(128, 128)]
    n_curve = lax.axis_size("curve")
    rightward = [(i, i + 1) for i in range(n_curve - 1)]
    leftward = [(i + 1, i) for i in range(n_curve - 1)]

    def exchange(left, right, tile):
        arrived = lax.all_to_all(
            tile.reshape(8, 16, 128), "tile", split_axis=0, concat_axis=0, tiled=True
        )
        from_left = lax.ppermute(right, "curve", rightward)
        from_right = lax.ppermute(left, "curve", leftward)
        return from_left, from_right, arrived.reshape(128, 128)

    numbers = [
        levels, send_faces.T, send_counts, recv_faces.T, recv_orients.T, recv_counts,
        curve_faces, curve_orients, curve_counts,
    ]
    u, left, right, own, tile, slots, masks = call(
        first_kernel,
        "first",
        out_shape=[shape(1024, 128), *payload, shape(288, kind=i32), shape(48, 128)],
        in_specs=[hbm] * 12,
        out_specs=[vmem] * 4 + [hbm, smem, vmem],
        scratch_shapes=[pltpu.SMEM(x.shape, i32) for x in numbers]
        + [
            pltpu.VMEM(state.shape, f32),
            pltpu.VMEM(index.shape, i32),
            pltpu.VMEM((384, 512), bf16),
            pltpu.VMEM((128, 128), f32),
            pltpu.VMEM((128, 128), f32),
            pltpu.SemaphoreType.DMA((13,)),
        ],
    )(*[pltpu.with_memory_space_constraint(x, pltpu.HBM) for x in (state, *numbers, index, mats)])
    scratch = [pltpu.VMEM((1024, 128), f32), pltpu.VMEM((128, 128), f32), pltpu.SMEM((288,), i32)]
    sems = pltpu.SemaphoreType.DMA((2,))
    kept = []
    for section in range(3):
        from_left, from_right, arrived = exchange(left, right, tile)
        if section == 0:
            faces, scale = call(
                faces_kernel,
                "faces",
                out_shape=[shape(352, 128), shape(256, 128)],
                in_specs=[smem],
                out_specs=[vmem] * 2,
                scratch_shapes=[pltpu.VMEM((200, 128), f32)],
                cost_estimate=pl.CostEstimate(
                    flops=20_000_000, bytes_accessed=1_000_000, transcendentals=0
                ),
            )(slots)
        args = (
            slots, u, from_left, from_right, arrived, own, masks, faces, scale,
            index, mats, coefs,
        )
        if section < 2:
            u, left, right, own, tile = call(
                next_kernel,
                "next",
                out_shape=[shape(1024, 128), *payload],
                in_specs=[anywhere] + [vmem] * 11,
                out_specs=[vmem] * 4 + [hbm],
                scratch_shapes=[*scratch, pltpu.VMEM((128, 128), f32), sems],
            )(*args)
            kept.append(u)
    return call(
        last_kernel,
        "last",
        out_shape=shape(5, 32, 512),
        in_specs=[anywhere] + [vmem] * 13,
        out_specs=vmem,
        scratch_shapes=[*scratch, sems],
    )(*args, state, kept[0])


def solution(mesh):
    both = P(("curve", "tile"))
    rows = P(("curve", "tile"), None)
    return jax.shard_map(
        shards,
        mesh=mesh,
        in_specs=(P(None, ("curve", "tile"), None), both, rows, both, rows, rows, both, rows, rows, both),
        out_specs=P(None, ("curve", "tile"), None),
        check_vma=False,
    )
```

time: 883 us -> 69.8 us (0.08); the launches traced: 871 us -> 68.8 us
  local copies, waits for them, and re-layouts: 691 us -> 0.02 us
  other arithmetic: 63.5 us -> 0 us
  matrix products: 30 us -> 0 us
  starting transfers between devices: 67.2 us -> 52.6 us
  waiting for transfers between devices: 16.6 us -> 4.08 us
  Pallas kernels: 0 us -> 12 us
    gather x43 -> x0, local copies, waits for them, and re-layouts: 603 us -> none  [the longest x28 585 us: orient(): jnp.take_along_axis(values, jnp.broadcast_to(gather_index[None], values.s...]
    dot_general x21 -> x0, matrix products: 30 us -> none  [the longest x3 6.54 us: spread_faces(): jnp.dot(jump_term.reshape(fields * elements, 384), selector.T, precision=...]
    scatter-add x12 -> x0, other arithmetic: 23.7 us -> none  [the longest x3 9.4 us: rhs(): accumulated = accumulated.at[:, curve_ids].add(curve_flux)]
    reshape x31 -> x0, local copies, waits for them, and re-layouts: 22.3 us -> none  [the longest x9 10.1 us: face_traces(): return flat.reshape(fields, elements * 6, 64)]
    slice x32 -> x0, local copies, waits for them, and re-layouts: 20 us -> none  [the longest x9 8.36 us: wall_state(): own_side[:1]]
    all_to_all x6 -> x3, waiting for transfers between devices: 16.6 us -> 0.01 us  [exchange(): lax.all_to_all(tile.reshape(8, 16, 128), 'tile', split_axis=0, concat_axi...]
    all_to_all x6 -> x3, starting transfers between devices: 35.7 us -> 21.4 us  [exchange(): lax.all_to_all(tile.reshape(8, 16, 128), 'tile', split_axis=0, concat_axi...]
    unnamed x387 -> x8, local copies, waits for them, and re-layouts: 13.6 us -> 0.02 us
  transfers between devices with their start and end apart: 12 -> 9, of which waited for: 3 -> 3; matrix products, arithmetic and copies ran while one was open for 77% -> 0% of each run, Pallas kernels for 0% -> 1%
where the time goes in v1:
time: 69.8 us; the launch traced here: 68.8 us
  starting transfers between devices  52.6 us (75%)
  Pallas kernels  12 us (17%)
  waiting for transfers between devices  4.08 us (6%)
    ppermute x3, starting transfers between devices, exchange(): from_right = lax.ppermute(left, 'curve', leftward)  25.5 us
    all_to_all x3, starting transfers between devices, exchange(): lax.all_to_all(tile.reshape(8, 16, 128), 'tile', split_axis=0, concat_axi...  21.4 us
    ppermute x3, starting transfers between devices, exchange(): from_left = lax.ppermute(right, 'curve', rightward)  5.73 us
    pallas_call x2, Pallas kernels, shards(): call(next_kernel, 'next', out_shape=[shape(1024, 128), *payload], in_spec...  5.25 us
    ppermute x3, waiting for transfers between devices, exchange(): from_right = lax.ppermute(left, 'curve', leftward)  4.07 us
    pallas_call x1, Pallas kernels, shards(): call(first_kernel, 'first', out_shape=[shape(1024, 128), *payload, shape(...  3.62 us
    pallas_call x1, Pallas kernels, shards(): call(last_kernel, 'last', out_shape=shape(5, 32, 512), in_specs=[anywhere...  2.5 us
  transfers between devices with their start and end apart: 9, of which 3 were waited for; matrix products, arithmetic and copies ran while one was open for 0% of the time, Pallas kernels for 1%

profile of v1, /device:TPU:6, one launch (start us, length us, event | category | flops | bytes accessed | tf_op | source)
XLA Modules:
  0.0 68.8 jit_solution(8187405679716925262)
XLA Ops:
  0.0 0.0 copy-start
  0.0 0.0 copy-start.3
  0.0 3.6 %first.1 = (f32[1024,128]{1,0:T(8,128)S(1)}, f32[64,128]{1,0:T(8,128)S(1)}, f32[64,128]{1,0:T(8,128)S(1)}, f32[64,128]{1,0:T(8,128)S(1)}, f32[128,128]{1,0:T(8,1...) custom-call(f32[5,32,512]{2,1,0:T(8,128)} %state_ref.1, s32[32]{0:T(128)} %levels_hbm.1, s32[2,8]{1,0:T(2,128)} %bitcast.12, ...), custom_call_target="tpu_custom_call" | custom-call | tf_op jit(solution)/shard_map/first/pallas_call | solution.py:541
  3.6 0.0 copy-start.1
  3.6 7.2 %all-to-all-start = ((f32[8,16,128]{2,1,0:T(8,128)}), f32[8,16,128]{2,1,0:T(8,128)S(1)}, u32[]{:S(2)}, u32[]{:S(2)}) async-start(f32[8,16,128]{2,1,0:T(8,128)} %bitcast.3), calls=%async_computation | async-start | bytes 131072 | tf_op jit(solution)/shard_map/all_to_all | solution.py:530
  10.9 1.9 %collective-permute-start = (f32[64,128]{1,0:T(8,128)S(1)}, f32[64,128]{1,0:T(8,128)S(1)}, u32[]{:S(2)}, u32[]{:S(2)}) collective-permute-start(f32[64,128]{1,0:T(8,128)S(1)} %get-tuple-element.26), channel_id=1, source_target_pairs={{0,8},{8,16},{16,24},{24,32},{32,40},{40,48},{48,56},{56,64},{64,7... | collective-permute-start | bytes 98312 | tf_op jit(solution)/shard_map/ppermute | solution.py:533
  12.8 14.0 %collective-permute-start.1 = (f32[64,128]{1,0:T(8,128)S(1)}, f32[64,128]{1,0:T(8,128)S(1)}, u32[]{:S(2)}, u32[]{:S(2)}) collective-permute-start(f32[64,128]{1,0:T(8,128)S(1)} %get-tuple-element.27), channel_id=1, source_target_pairs={{8,0},{16,8},{24,16},{32,24},{40,32},{48,40},{56,48},{64,56},{72,6... | collective-permute-start | bytes 98312 | tf_op jit(solution)/shard_map/ppermute | solution.py:534
  26.8 0.6 faces.1
  27.5 0.0 collective-permute-done.from_left
  27.5 0.9 %collective-permute-done.1.from_right = f32[64,128]{1,0:T(8,128)S(1)} collective-permute-done((f32[64,128]{1,0:T(8,128)S(1)}, f32[64,128]{1,0:T(8,128)S(1)}, u32[]{:S(2)}, u32[]{:S(2)}) %collective-permute-start.1) | collective-permute-done | bytes 32800 | tf_op jit(solution)/shard_map/ppermute | solution.py:534
  28.4 0.0 all-to-all-done
  28.4 0.0 copy-done
  28.4 0.0 copy-done.3
  28.4 0.0 copy-done.1
  28.4 2.6 %next.2 = (f32[1024,128]{1,0:T(8,128)S(1)}, f32[64,128]{1,0:T(8,128)S(1)}, f32[64,128]{1,0:T(8,128)S(1)}, f32[64,128]{1,0:T(8,128)S(1)}, f32[128,128]{1,0:T(8,128)}) custom-call(s32[288]{0:T(512)S(1)} %get-tuple-element.24.slots.slots_any, f32[1024,128]{1,0:T(8,128)S(1)} %get-tuple-element.25.u_ref, f32[64,128]{1,0:T(8,128)S(1)} %collective-permute-done.from_left, ...), custom_call_target="tpu_custom_call" | custom-call | tf_op jit(solution)/shard_map/next/pallas_call | solution.py:579
  31.0 6.9 %all-to-all-start.1 = ((f32[8,16,128]{2,1,0:T(8,128)}), f32[8,16,128]{2,1,0:T(8,128)S(1)}, u32[]{:S(2)}, u32[]{:S(2)}) async-start(f32[8,16,128]{2,1,0:T(8,128)} %bitcast.5), calls=%async_computation.1 | async-start | bytes 131072 | tf_op jit(solution)/shard_map/all_to_all | solution.py:530
  38.0 1.9 %collective-permute-start.2 = (f32[64,128]{1,0:T(8,128)S(1)}, f32[64,128]{1,0:T(8,128)S(1)}, u32[]{:S(2)}, u32[]{:S(2)}) collective-permute-start(f32[64,128]{1,0:T(8,128)S(1)} %get-tuple-element.34), channel_id=1, source_target_pairs={{0,8},{8,16},{16,24},{24,32},{32,40},{40,48},{48,56},{56,64},{64,7... | collective-permute-start | bytes 98312 | tf_op jit(solution)/shard_map/ppermute | solution.py:533
  39.9 5.8 %collective-permute-start.3 = (f32[64,128]{1,0:T(8,128)S(1)}, f32[64,128]{1,0:T(8,128)S(1)}, u32[]{:S(2)}, u32[]{:S(2)}) collective-permute-start(f32[64,128]{1,0:T(8,128)S(1)} %get-tuple-element.35), channel_id=1, source_target_pairs={{8,0},{16,8},{24,16},{32,24},{40,32},{48,40},{56,48},{64,56},{72,6... | collective-permute-start | bytes 98312 | tf_op jit(solution)/shard_map/ppermute | solution.py:534
  45.6 0.0 collective-permute-done.2.from_left
  45.7 1.6 %collective-permute-done.3.from_right = f32[64,128]{1,0:T(8,128)S(1)} collective-permute-done((f32[64,128]{1,0:T(8,128)S(1)}, f32[64,128]{1,0:T(8,128)S(1)}, u32[]{:S(2)}, u32[]{:S(2)}) %collective-permute-start.3) | collective-permute-done | bytes 32800 | tf_op jit(solution)/shard_map/ppermute | solution.py:534
  47.2 0.0 all-to-all-done.1
  47.2 0.0 copy-start.2
  47.2 2.6 %next.3 = (f32[1024,128]{1,0:T(8,128)S(1)}, f32[64,128]{1,0:T(8,128)S(1)}, f32[64,128]{1,0:T(8,128)S(1)}, f32[64,128]{1,0:T(8,128)S(1)}, f32[128,128]{1,0:T(8,128)}) custom-call(s32[288]{0:T(512)S(1)} %get-tuple-element.24.slots.slots_any, f32[1024,128]{1,0:T(8,128)S(1)} %get-tuple-element.33.u_ref.first_ref, ...), custom_call_target="tpu_custom_call" | custom-call | tf_op jit(solution)/shard_map/next/pallas_call | solution.py:579
  49.9 7.2 %all-to-all-start.2 = ((f32[8,16,128]{2,1,0:T(8,128)}), f32[8,16,128]{2,1,0:T(8,128)S(1)}, u32[]{:S(2)}, u32[]{:S(2)}) async-start(f32[8,16,128]{2,1,0:T(8,128)} %bitcast.7), calls=%async_computation.2 | async-start | bytes 131072 | tf_op jit(solution)/shard_map/all_to_all | solution.py:530
  57.1 1.9 %collective-permute-start.4 = (f32[64,128]{1,0:T(8,128)S(1)}, f32[64,128]{1,0:T(8,128)S(1)}, u32[]{:S(2)}, u32[]{:S(2)}) collective-permute-start(f32[64,128]{1,0:T(8,128)S(1)} %get-tuple-element.39), channel_id=1, source_target_pairs={{0,8},{8,16},{16,24},{24,32},{32,40},{40,48},{48,56},{56,64},{64,7... | collective-permute-start | bytes 98312 | tf_op jit(solution)/shard_map/ppermute | solution.py:533
  59.0 5.8 %collective-permute-start.5 = (f32[64,128]{1,0:T(8,128)S(1)}, f32[64,128]{1,0:T(8,128)S(1)}, u32[]{:S(2)}, u32[]{:S(2)}) collective-permute-start(f32[64,128]{1,0:T(8,128)S(1)} %get-tuple-element.40), channel_id=1, source_target_pairs={{8,0},{16,8},{24,16},{32,24},{40,32},{48,40},{56,48},{64,56},{72,6... | collective-permute-start | bytes 98312 | tf_op jit(solution)/shard_map/ppermute | solution.py:534
  64.7 0.0 collective-permute-done.4.from_left
  64.8 1.6 %collective-permute-done.5.from_right = f32[64,128]{1,0:T(8,128)S(1)} collective-permute-done((f32[64,128]{1,0:T(8,128)S(1)}, f32[64,128]{1,0:T(8,128)S(1)}, u32[]{:S(2)}, u32[]{:S(2)}) %collective-permute-start.5) | collective-permute-done | bytes 32800 | tf_op jit(solution)/shard_map/ppermute | solution.py:534
  66.3 0.0 all-to-all-done.2
  66.3 0.0 copy-done.2
  66.3 2.5 %last.1 = f32[5,32,512]{2,1,0:T(8,128)} custom-call(s32[288]{0:T(512)S(1)} %get-tuple-element.24.slots.slots_any, f32[1024,128]{1,0:T(8,128)S(1)} %get-tuple-element.38.u_ref, f32[64,128]{1,0:T(8,128)S(1)} %collective-permute-done.4.from_left, f32[64,128]{1,0:T(8,128)S(1)} %collective-permute-done.5.from_right, f32[128,128]{1,0:T(8,128)S(1)} %bitcast.9, ...), custom_call_target="tpu_custom_call" | custom-call | tf_op jit(solution)/shard_map/last/pallas_call | solution.py:588
Async XLA Ops:
  0.0 28.4 %copy-start = (bf16[1024,512]{1,0:T(8,128)(2,1)S(1)}, bf16[1024,512]{1,0:T(8,128)(2,1)}, u32[]{:S(2)}) copy-start(bf16[1024,512]{1,0:T(8,128)(2,1)} %constant.19.mats_hbm.mats_ref) | copy-start | bytes 3145732
  0.0 28.4 %copy-start.3 = (f32[32,128]{1,0:T(8,128)S(1)}, f32[32,128]{1,0:T(8,128)}, u32[]{:S(2)}) copy-start(f32[32,128]{1,0:T(8,128)} %constant.8.clone.coefs_ref) | copy-start | bytes 49156
  3.6 24.8 %copy-start.1 = (s32[416,128]{1,0:T(8,128)S(1)}, s32[416,128]{1,0:T(8,128)}, u32[]{:S(2)}) copy-start(s32[416,128]{1,0:T(8,128)} %constant.6.clone.index_hbm.index_ref) | copy-start | bytes 638980
  3.6 24.8 %all-to-all-start = ((f32[8,16,128]{2,1,0:T(8,128)}), f32[8,16,128]{2,1,0:T(8,128)S(1)}, u32[]{:S(2)}, u32[]{:S(2)}) async-start(f32[8,16,128]{2,1,0:T(8,128)} %bitcast.3), calls=%async_computation | async-start | bytes 131072 | tf_op jit(solution)/shard_map/all_to_all | solution.py:530
  10.9 16.6 %collective-permute-start = (f32[64,128]{1,0:T(8,128)S(1)}, f32[64,128]{1,0:T(8,128)S(1)}, u32[]{:S(2)}, u32[]{:S(2)}) collective-permute-start(f32[64,128]{1,0:T(8,128)S(1)} %get-tuple-element.26), channel_id=1, source_target_pairs={{0,8},{8,16},{16,24},{24,32},{32,40},{40,48},{48,56},{56,64},{64,7... | collective-permute-start | bytes 98312 | tf_op jit(solution)/shard_map/ppermute | solution.py:533
  12.8 15.6 %collective-permute-start.1 = (f32[64,128]{1,0:T(8,128)S(1)}, f32[64,128]{1,0:T(8,128)S(1)}, u32[]{:S(2)}, u32[]{:S(2)}) collective-permute-start(f32[64,128]{1,0:T(8,128)S(1)} %get-tuple-element.27), channel_id=1, source_target_pairs={{8,0},{16,8},{24,16},{32,24},{40,32},{48,40},{56,48},{64,56},{72,6... | collective-permute-start | bytes 98312 | tf_op jit(solution)/shard_map/ppermute | solution.py:534
  31.0 16.2 %all-to-all-start.1 = ((f32[8,16,128]{2,1,0:T(8,128)}), f32[8,16,128]{2,1,0:T(8,128)S(1)}, u32[]{:S(2)}, u32[]{:S(2)}) async-start(f32[8,16,128]{2,1,0:T(8,128)} %bitcast.5), calls=%async_computation.1 | async-start | bytes 131072 | tf_op jit(solution)/shard_map/all_to_all | solution.py:530
  38.0 7.7 %collective-permute-start.2 = (f32[64,128]{1,0:T(8,128)S(1)}, f32[64,128]{1,0:T(8,128)S(1)}, u32[]{:S(2)}, u32[]{:S(2)}) collective-permute-start(f32[64,128]{1,0:T(8,128)S(1)} %get-tuple-element.34), channel_id=1, source_target_pairs={{0,8},{8,16},{16,24},{24,32},{32,40},{40,48},{48,56},{56,64},{64,7... | collective-permute-start | bytes 98312 | tf_op jit(solution)/shard_map/ppermute | solution.py:533
  39.9 7.3 %collective-permute-start.3 = (f32[64,128]{1,0:T(8,128)S(1)}, f32[64,128]{1,0:T(8,128)S(1)}, u32[]{:S(2)}, u32[]{:S(2)}) collective-permute-start(f32[64,128]{1,0:T(8,128)S(1)} %get-tuple-element.35), channel_id=1, source_target_pairs={{8,0},{16,8},{24,16},{32,24},{40,32},{48,40},{56,48},{64,56},{72,6... | collective-permute-start | bytes 98312 | tf_op jit(solution)/shard_map/ppermute | solution.py:534
  47.2 19.1 %copy-start.2 = (f32[5,32,512]{2,1,0:T(8,128)S(1)}, f32[5,32,512]{2,1,0:T(8,128)}, u32[]{:S(2)}) copy-start(f32[5,32,512]{2,1,0:T(8,128)} %state_ref.1) | copy-start | bytes 983044
  49.9 16.5 %all-to-all-start.2 = ((f32[8,16,128]{2,1,0:T(8,128)}), f32[8,16,128]{2,1,0:T(8,128)S(1)}, u32[]{:S(2)}, u32[]{:S(2)}) async-start(f32[8,16,128]{2,1,0:T(8,128)} %bitcast.7), calls=%async_computation.2 | async-start | bytes 131072 | tf_op jit(solution)/shard_map/all_to_all | solution.py:530
  57.1 7.7 %collective-permute-start.4 = (f32[64,128]{1,0:T(8,128)S(1)}, f32[64,128]{1,0:T(8,128)S(1)}, u32[]{:S(2)}, u32[]{:S(2)}) collective-permute-start(f32[64,128]{1,0:T(8,128)S(1)} %get-tuple-element.39), channel_id=1, source_target_pairs={{0,8},{8,16},{16,24},{24,32},{32,40},{40,48},{48,56},{56,64},{64,7... | collective-permute-start | bytes 98312 | tf_op jit(solution)/shard_map/ppermute | solution.py:533
  59.0 7.3 %collective-permute-start.5 = (f32[64,128]{1,0:T(8,128)S(1)}, f32[64,128]{1,0:T(8,128)S(1)}, u32[]{:S(2)}, u32[]{:S(2)}) collective-permute-start(f32[64,128]{1,0:T(8,128)S(1)} %get-tuple-element.40), channel_id=1, source_target_pairs={{8,0},{16,8},{24,16},{32,24},{40,32},{48,40},{56,48},{64,56},{72,6... | collective-permute-start | bytes 98312 | tf_op jit(solution)/shard_map/ppermute | solution.py:534

commit v2 on v1

--- a/solution.py
+++ b/solution.py
@@ -190,7 +190,7 @@
             out_ref[pl.ds(f, 8, stride=8), :] = parts[f]
 
 
-def pack_tile(u_ref, slots, masks_ref, index_ref, mats_ref, tmp, own_ref, tile_ref):
+def pack_tile(u_ref, slots, masks_ref, index_ref, mats_ref, tmp, own_ref, tile_ref, ready=None):
     low = lanes() < 64
     quarter = (lanes() % 64) // 16
     for side in range(2):
@@ -214,6 +214,8 @@
                 )
             tmp[64 * side + 8 * p : 64 * side + 8 * p + 8, :] = pair
     q = [tmp[pl.ds(f, 8, stride=8), :] for f in range(5)]
+    if ready is not None:
+        ready.wait()
     q = child_map(q, mats_ref, 0, masks_ref[CHILD : CHILD + 8, :])
     is_z = masks_ref[SEND_Z : SEND_Z + 8, :] > 0.0
     for f, part in enumerate(neighbour_part(q, -1.0, is_z, 14.0)):
@@ -226,18 +228,18 @@
         tile_ref[pl.ds(8 + f, 8, stride=16), :] = part
 
 
-def spread(w_ref, pair, slots, s, half, end, index_ref):
+def spread(w_refs, pair, slots, s, half, end, index_ref):
     kind = slots[128 + s]
     lane = lanes()
     position = jnp.where(kind == 0, (lane // 8) % 8, lane % 8)
     at_face = position == end
     for a in range(4):
         moved = take(pair, row(index_ref, kind * 64 + SPREAD + 32 * half + 8 * a))
-        block = pl.ds(pl.multiple_of(slots[s] + 256 * a, 8), 8)
-        w_ref[block, :] = w_ref[block, :] - jnp.where(at_face, moved, 0.0)
-
-
-def unpack(w_ref, slots, masks_ref, index_ref, mats_ref, tmp, from_left, from_right, tile_ref, own_ref):
+        block = pl.ds(pl.multiple_of(slots[s], 8), 8)
+        w_refs[a][block, :] = w_refs[a][block, :] - jnp.where(at_face, moved, 0.0)
+
+
+def unpack(w_refs, slots, masks_ref, index_ref, mats_ref, tmp, from_left, from_right, tile_ref, own_ref):
     low = lanes() < 64
     q = [
         tile_ref[pl.ds(8 + f, 8, stride=16), :] - own_ref[pl.ds(f, 8, stride=8), :]
@@ -251,7 +253,8 @@
             pair = in_ref[8 * k : 8 * k + 8, :]
             turned = pltpu.roll(pair, 64, 1)
             for s, value in ((k, (pair, turned)[side]), (k + 8, (turned, pair)[side])):
-                block = pl.ds(pl.multiple_of(slots[16 * side + s] + 768 * side, 8), 8)
+                w_ref = w_refs[3 * side]
+                block = pl.ds(pl.multiple_of(slots[16 * side + s], 8), 8)
                 kept = jnp.where(low, value, 0.0) if side == 0 else jnp.where(low, 0.0, value)
                 w_ref[block, :] = w_ref[block, :] - kept
     for p in range(8):
@@ -263,14 +266,14 @@
             take(pair, row(index_ref, slots[65 + s] + PERM + 64)),
         )
         for k in range(2):
-            spread(w_ref, pair, slots, s + k, k, 0, index_ref)
+            spread(w_refs, pair, slots, s + k, k, 0, index_ref)
     for p in range(8):
         pair = tmp[8 * p : 8 * p + 8, :]
         for k in range(2):
-            spread(w_ref, pair, slots, 32 + 2 * p + k, k, 7, index_ref)
-
-
-def inside(u_ref, faces_ref, mats_ref, coefs_ref, w_ref):
+            spread(w_refs, pair, slots, 32 + 2 * p + k, k, 7, index_ref)
+
+
+def inside(u_ref, faces_ref, mats_ref, coefs_ref, w_refs):
     fields = [[u_ref[pl.ds(256 * a + f, 32, stride=8), :] for a in range(4)] for f in range(5)]
     dens, vx, vy, vz, pres = fields
 
@@ -319,15 +322,15 @@
         out[2] = grad_y[4 + a] + uy0 * (p - y) - uy7 * (p + y) - (asum - ay) * y
         out[3] = grad_z[4 + a] + uz0 * (p - z) - uz7 * (p + z) - (asum - az) * z
         for f in range(5):
-            w_ref[pl.ds(256 * a + f, 32, stride=8), :] = out[f]
+            w_refs[a][pl.ds(f, 32, stride=8), :] = out[f]
 
 
 def first_kernel(
-    state_hbm, levels_hbm, send_faces_hbm, send_counts_hbm, recv_faces_hbm, recv_orients_hbm,
-    recv_counts_hbm, curve_faces_hbm, curve_orients_hbm, curve_counts_hbm, index_hbm, mats_hbm,
-    u_ref, left_ref, right_ref, own_ref, tile_hbm, slots, masks_ref,
-    levels, send_faces, send_counts, recv_faces, recv_orients, recv_counts, curve_faces,
-    curve_orients, curve_counts, state_ref, index_ref, mats_ref, tmp, tile_ref, sems,
+    state_hbm, send_faces_hbm, send_counts_hbm, recv_faces_hbm, recv_orients_hbm,
+    recv_counts_hbm, curve_faces_hbm, curve_orients_hbm, curve_counts_hbm, index_hbm, mats_hbm, coefs_hbm,
+    u_ref, left_ref, right_ref, own_ref, tile_hbm, slots_any, masks_ref, index_ref, mats_ref, coefs_ref,
+    send_faces, send_counts, recv_faces, recv_orients, recv_counts, curve_faces,
+    curve_orients, curve_counts, slots, state_ref, tmp, tile_ref, sems,
 ):
     numbers = [
         pltpu.make_async_copy(source, target, sems.at[n])
@@ -341,17 +344,18 @@
                 (recv_faces_hbm, recv_faces),
                 (recv_orients_hbm, recv_orients),
                 (recv_counts_hbm, recv_counts),
-                (levels_hbm, levels),
             )
         )
     ]
     arrays = [
-        pltpu.make_async_copy(source, target, sems.at[9 + n])
+        pltpu.make_async_copy(source, target, sems.at[8 + n])
         for n, (source, target) in enumerate(
             (
                 (state_hbm, state_ref),
                 (index_hbm, index_ref),
-                (mats_hbm.at[pl.ds(0, 384), :], mats_ref),
+                (mats_hbm.at[pl.ds(0, 384), :], mats_ref.at[pl.ds(0, 384), :]),
+                (mats_hbm.at[pl.ds(384, 640), :], mats_ref.at[pl.ds(384, 640), :]),
+                (coefs_hbm, coefs_ref),
             )
         )
     ]
@@ -372,8 +376,6 @@
             element = (curve_faces[side, k] * 10923) >> 16
             slots[s] = element * 8
             slots[64 + s] = curve_orients[side, k] * 8
-            slots[128 + s] = 0
-            slots[192 + s] = jnp.where(is_live, 32 * side + element, 192)
             live.append(jnp.where(is_live, 1.0, 0.0))
         for k in range(8):
             at = CURVE_LIVE + 8 * side + k
@@ -388,9 +390,7 @@
             rest = number - 30 * element
             is_z = rest >= 25
             slots[s] = element * 8
-            slots[64 + s] = 0
             slots[128 + s] = jnp.where(is_z, 1, 0)
-            slots[192 + s] = jnp.where(is_live, jnp.where(is_z, 160, 96) + element, 192)
             child.append(jnp.where(is_live, jnp.where(is_z, rest - 25, rest - 15), -1))
             kinds.append(jnp.where(is_z, 1.0, 0.0))
             s = 48 + 2 * p + k
@@ -401,34 +401,48 @@
             slots[s] = element * 8
             slots[64 + s] = recv_orients[k, p] * 8
             slots[128 + s] = jnp.where(is_z, 1, 0)
-            slots[192 + s] = jnp.where(is_live, jnp.where(is_z, 128, 64) + element, 192)
             recv_kinds.append(jnp.where(is_z, 1.0, 0.0))
             recv_live.append(jnp.where(is_live, 1.0, 0.0))
         masks_ref[CHILD + p : CHILD + p + 1, :] = halves(*child).astype(f32)
         masks_ref[SEND_Z + p : SEND_Z + p + 1, :] = halves(*kinds)
         masks_ref[RECV_Z + p : RECV_Z + p + 1, :] = halves(*recv_kinds)
         masks_ref[RECV_LIVE + p : RECV_LIVE + p + 1, :] = halves(*recv_live)
-    for e in range(32):
-        slots[256 + e] = 1 << levels[e]
-    for copy in arrays:
-        copy.wait()
+    keep = pltpu.make_async_copy(slots, slots_any, sems.at[13])
+    keep.start()
+    arrays[0].wait()
     for f in range(5):
         for a in range(4):
             u_ref[pl.ds(256 * a + f, 32, stride=8), :] = state_ref[f, :, 128 * a : 128 * a + 128]
-    pack_tile(u_ref, slots, masks_ref, index_ref, mats_ref, tmp, own_ref, tile_ref)
-    send = pltpu.make_async_copy(tile_ref, tile_hbm, sems.at[12])
+    arrays[1].wait()
+    pack_tile(
+        u_ref, slots, masks_ref, index_ref, mats_ref, tmp, own_ref, tile_ref, ready=arrays[2]
+    )
+    send = pltpu.make_async_copy(tile_ref, tile_hbm, sems.at[14])
     send.start()
     pack_curve(u_ref, slots, masks_ref, index_ref, tmp, left_ref, right_ref)
-    send.wait()
-
-
-def faces_kernel(slots, faces_ref, scale_ref, listed):
+    for copy in (*arrays[3:], keep, send):
+        copy.wait()
+
+
+def faces_kernel(
+    slots, levels, send_counts, recv_counts, curve_counts, faces_ref, scale_ref, listed
+):
     listed[...] = jnp.zeros_like(listed)
     for s in range(64):
-        listed[pl.ds(slots[192 + s], 1), :] = jnp.ones((1, 128), f32)
+        element = slots[s] >> 3
+        if s < 32:
+            is_live = s % 16 < curve_counts[s // 16]
+            at = 32 * (s // 16) + element
+        elif s < 48:
+            is_live = s % 2 < send_counts[s % 16 // 2]
+            at = 96 + 64 * slots[128 + s] + element
+        else:
+            is_live = s % 2 < recv_counts[s % 16 // 2]
+            at = 64 + 64 * slots[128 + s] + element
+        listed[pl.ds(jnp.where(is_live, at, 192), 1), :] = jnp.ones((1, 128), f32)
     for e in range(32):
         scale_ref[8 * e : 8 * e + 8, :] = (
-            jnp.full((8, 128), slots[256 + e], i32).astype(f32) * time_step
+            jnp.full((8, 128), 1 << levels[e], i32).astype(f32) * time_step
         )
     lane = lax.broadcasted_iota(i32, (32, 128), 1)
     on = [listed[32 * f : 32 * f + 32, :] for f in range(6)]
@@ -460,17 +474,18 @@
 def next_kernel(
     slots_any, u_ref, from_left, from_right, arrived_ref, sent_ref, masks_ref, faces_ref, scale_ref,
     index_ref, mats_ref, coefs_ref,
-    out_ref, left_ref, right_ref, own_ref, tile_hbm, w_ref, tmp, slots, tile_ref, sems,
+    out_ref, left_ref, right_ref, own_ref, tile_hbm, w_0, w_1, w_2, w_3, tmp, slots, tile_ref, sems,
 ):
+    w_refs = (w_0, w_1, w_2, w_3)
     fetch = pltpu.make_async_copy(slots_any, slots, sems.at[0])
     fetch.start()
-    inside(u_ref, faces_ref, mats_ref, coefs_ref, w_ref)
+    inside(u_ref, faces_ref, mats_ref, coefs_ref, w_refs)
     fetch.wait()
     unpack(
-        w_ref, slots, masks_ref, index_ref, mats_ref, tmp, from_left, from_right, arrived_ref, sent_ref
+        w_refs, slots, masks_ref, index_ref, mats_ref, tmp, from_left, from_right, arrived_ref, sent_ref
     )
     for a in range(4):
-        out_ref[256 * a : 256 * a + 256, :] = w_ref[256 * a : 256 * a + 256, :] * scale_ref[...]
+        out_ref[256 * a : 256 * a + 256, :] = w_refs[a][...] * scale_ref[...]
     pack_tile(out_ref, slots, masks_ref, index_ref, mats_ref, tmp, own_ref, tile_ref)
     send = pltpu.make_async_copy(tile_ref, tile_hbm, sems.at[1])
     send.start()
@@ -481,14 +496,15 @@
 def last_kernel(
     slots_any, u_ref, from_left, from_right, arrived_ref, sent_ref, masks_ref, faces_ref, scale_ref,
     index_ref, mats_ref, coefs_ref, state_ref, first_ref,
-    out_ref, w_ref, tmp, slots, sems,
+    out_ref, w_0, w_1, w_2, w_3, tmp, slots, sems,
 ):
+    w_refs = (w_0, w_1, w_2, w_3)
     fetch = pltpu.make_async_copy(slots_any, slots, sems.at[0])
     fetch.start()
-    inside(u_ref, faces_ref, mats_ref, coefs_ref, w_ref)
+    inside(u_ref, faces_ref, mats_ref, coefs_ref, w_refs)
     fetch.wait()
     unpack(
-        w_ref, slots, masks_ref, index_ref, mats_ref, tmp, from_left, from_right, arrived_ref, sent_ref
+        w_refs, slots, masks_ref, index_ref, mats_ref, tmp, from_left, from_right, arrived_ref, sent_ref
     )
     scale = scale_ref[pl.ds(0, 32, stride=8), :] * (1.0 / 6.0)
     for f in range(5):
@@ -496,7 +512,10 @@
             at = (pl.ds(256 * a + f, 32, stride=8), slice(None))
             column = slice(128 * a, 128 * a + 128)
             out_ref[f, :, column] = (
-                state_ref[f, :, column] + first_ref[at] + 0.5 * u_ref[at] + w_ref[at] * scale
+                state_ref[f, :, column]
+                + first_ref[at]
+                + 0.5 * u_ref[at]
+                + w_refs[a][pl.ds(f, 32, stride=8), :] * scale
             )
 
 
@@ -535,26 +554,26 @@
         return from_left, from_right, arrived.reshape(128, 128)
 
     numbers = [
-        levels, send_faces.T, send_counts, recv_faces.T, recv_orients.T, recv_counts,
+        send_faces.T, send_counts, recv_faces.T, recv_orients.T, recv_counts,
         curve_faces, curve_orients, curve_counts,
     ]
-    u, left, right, own, tile, slots, masks = call(
+    u, left, right, own, tile, slots, masks, index, mats, coefs = call(
         first_kernel,
         "first",
-        out_shape=[shape(1024, 128), *payload, shape(288, kind=i32), shape(48, 128)],
+        out_shape=[shape(1024, 128), *payload, shape(256, kind=i32), shape(48, 128)]
+        + [shape(*x.shape, kind=x.dtype) for x in (index, mats, coefs)],
         in_specs=[hbm] * 12,
-        out_specs=[vmem] * 4 + [hbm, smem, vmem],
-        scratch_shapes=[pltpu.SMEM(x.shape, i32) for x in numbers]
+        out_specs=[vmem] * 4 + [hbm, anywhere] + [vmem] * 4,
+        scratch_shapes=[pltpu.SMEM(x.shape, i32) for x in numbers] + [pltpu.SMEM((256,), i32)]
         + [
             pltpu.VMEM(state.shape, f32),
-            pltpu.VMEM(index.shape, i32),
-            pltpu.VMEM((384, 512), bf16),
             pltpu.VMEM((128, 128), f32),
             pltpu.VMEM((128, 128), f32),
-            pltpu.SemaphoreType.DMA((13,)),
+            pltpu.SemaphoreType.DMA((15,)),
         ],
-    )(*[pltpu.with_memory_space_constraint(x, pltpu.HBM) for x in (state, *numbers, index, mats)])
-    scratch = [pltpu.VMEM((1024, 128), f32), pltpu.VMEM((128, 128), f32), pltpu.SMEM((288,), i32)]
+    )(*[pltpu.with_memory_space_constraint(x, pltpu.HBM) for x in (state, *numbers, index, mats, coefs)])
+    scratch = [pltpu.VMEM((256, 128), f32)] * 4
+    scratch += [pltpu.VMEM((128, 128), f32), pltpu.SMEM((256,), i32)]
     sems = pltpu.SemaphoreType.DMA((2,))
     kept = []
     for section in range(3):
@@ -564,13 +583,13 @@
                 faces_kernel,
                 "faces",
                 out_shape=[shape(352, 128), shape(256, 128)],
-                in_specs=[smem],
+                in_specs=[smem] * 5,
                 out_specs=[vmem] * 2,
                 scratch_shapes=[pltpu.VMEM((200, 128), f32)],
                 cost_estimate=pl.CostEstimate(
                     flops=20_000_000, bytes_accessed=1_000_000, transcendentals=0
                 ),
-            )(slots)
+            )(slots, levels, send_counts, recv_counts, curve_counts)
         args = (
             slots, u, from_left, from_right, arrived, own, masks, faces, scale,
             index, mats, coefs,

time: 69.8 us -> 68.5 us (0.981)
  Pallas kernels: 12 us -> 10.8 us
    pallas_call x1, Pallas kernels: 3.62 us -> 2.77 us  [shards(): call(first_kernel, 'first', out_shape=[shape(1024, 128), *payload, shape(...]
where the time goes in v2:
time: 68.5 us; the launch traced here: 67.6 us
  starting transfers between devices  52.6 us (77%)
  Pallas kernels  10.8 us (16%)
  waiting for transfers between devices  3.92 us (6%)
    ppermute x3, starting transfers between devices, exchange(): from_right = lax.ppermute(left, 'curve', leftward)  25.6 us
    all_to_all x3, starting transfers between devices, exchange(): lax.all_to_all(tile.reshape(8, 16, 128), 'tile', split_axis=0, concat_axi...  21.3 us
    ppermute x3, starting transfers between devices, exchange(): from_left = lax.ppermute(right, 'curve', rightward)  5.73 us
    pallas_call x2, Pallas kernels, shards(): call(next_kernel, 'next', out_shape=[shape(1024, 128), *payload], in_spec...  4.99 us
    ppermute x3, waiting for transfers between devices, exchange(): from_right = lax.ppermute(left, 'curve', leftward)  3.91 us
    pallas_call x1, Pallas kernels, shards(): call(first_kernel, 'first', out_shape=[shape(1024, 128), *payload, shape(...  2.77 us
    pallas_call x1, Pallas kernels, shards(): call(last_kernel, 'last', out_shape=shape(5, 32, 512), in_specs=[anywhere...  2.32 us
  transfers between devices with their start and end apart: 9, of which 3 were waited for; matrix products, arithmetic and copies ran while one was open for 0% of the time, Pallas kernels for 1%

profile of v2, /device:TPU:6, one launch (start us, length us, event | category | flops | bytes accessed | tf_op | source)
XLA Modules:
  0.0 67.6 jit_solution(6152539265035003816)
XLA Ops:
  0.0 2.8 %first.1 = (f32[1024,128]{1,0:T(8,128)S(1)}, f32[64,128]{1,0:T(8,128)S(1)}, f32[64,128]{1,0:T(8,128)S(1)}, f32[64,128]{1,0:T(8,128)S(1)}, f32[128,128]{1,0:T(8,1...) custom-call(f32[5,32,512]{2,1,0:T(8,128)} %state_ref.1, ...), custom_call_target="tpu_custom_call" | custom-call | tf_op jit(solution)/shard_map/first/pallas_call | solution.py:560
  2.8 7.1 %all-to-all-start = ((f32[8,16,128]{2,1,0:T(8,128)}), f32[8,16,128]{2,1,0:T(8,128)S(1)}, u32[]{:S(2)}, u32[]{:S(2)}) async-start(f32[8,16,128]{2,1,0:T(8,128)} %bitcast.3), calls=%async_computation | async-start | bytes 131072 | tf_op jit(solution)/shard_map/all_to_all | solution.py:549
  9.9 1.9 %collective-permute-start = (f32[64,128]{1,0:T(8,128)S(1)}, f32[64,128]{1,0:T(8,128)S(1)}, u32[]{:S(2)}, u32[]{:S(2)}) collective-permute-start(f32[64,128]{1,0:T(8,128)S(1)} %get-tuple-element.29), channel_id=1, source_target_pairs={{0,8},{8,16},{16,24},{24,32},{32,40},{40,48},{48,56},{56,64},{64,7... | collective-permute-start | bytes 98312 | tf_op jit(solution)/shard_map/ppermute | solution.py:552
  11.8 0.0 copy-start.4
  11.8 0.0 copy-start.1
  11.8 0.0 copy-start.2
  11.8 0.0 copy-start.3
  11.9 14.1 %collective-permute-start.1 = (f32[64,128]{1,0:T(8,128)S(1)}, f32[64,128]{1,0:T(8,128)S(1)}, u32[]{:S(2)}, u32[]{:S(2)}) collective-permute-start(f32[64,128]{1,0:T(8,128)S(1)} %get-tuple-element.30), channel_id=1, source_target_pairs={{8,0},{16,8},{24,16},{32,24},{40,32},{48,40},{56,48},{64,56},{72,6... | collective-permute-start | bytes 98312 | tf_op jit(solution)/shard_map/ppermute | solution.py:553
  26.0 0.0 copy-done.4
  26.0 0.0 copy-done.1
  26.0 0.0 copy-done.2
  26.0 0.0 copy-done.3
  26.0 0.7 %faces.1 = (f32[352,128]{1,0:T(8,128)S(1)}, f32[256,128]{1,0:T(8,128)S(1)}) custom-call(s32[256]{0:T(256)S(1)} %get-tuple-element.27.slots.slots_any, s32[32]{0:T(128)S(1)} %copy-done.4, s32[8]{0:T(128)S(1)} %copy-done.1, s32[8]{0:T(128)S(1)} %copy-done.2, s32[2]{0:T(128)S(1)} %copy-done.3), custom_call_target="tpu_custom_call" | custom-call | flops 20000000 | bytes 1000000 | tf_op jit(solution)/shard_map/faces/pallas_call | solution.py:582
  26.8 0.0 collective-permute-done.from_left
  26.8 0.8 %collective-permute-done.1.from_right = f32[64,128]{1,0:T(8,128)S(1)} collective-permute-done((f32[64,128]{1,0:T(8,128)S(1)}, f32[64,128]{1,0:T(8,128)S(1)}, u32[]{:S(2)}, u32[]{:S(2)}) %collective-permute-start.1) | collective-permute-done | bytes 32800 | tf_op jit(solution)/shard_map/ppermute | solution.py:553
  27.6 0.0 all-to-all-done
  27.6 2.5 %next.2 = (f32[1024,128]{1,0:T(8,128)S(1)}, f32[64,128]{1,0:T(8,128)S(1)}, f32[64,128]{1,0:T(8,128)S(1)}, f32[64,128]{1,0:T(8,128)S(1)}, f32[128,128]{1,0:T(8,128)}) custom-call(s32[256]{0:T(256)S(1)} %get-tuple-element.27.slots.slots_any, f32[1024,128]{1,0:T(8,128)S(1)} %get-tuple-element.28.u_ref, f32[64,128]{1,0:T(8,128)S(1)} %collective-permute-done.from_left, ...), custom_call_target="tpu_custom_call" | custom-call | tf_op jit(solution)/shard_map/next/pallas_call | solution.py:598
  30.1 6.9 %all-to-all-start.1 = ((f32[8,16,128]{2,1,0:T(8,128)}), f32[8,16,128]{2,1,0:T(8,128)S(1)}, u32[]{:S(2)}, u32[]{:S(2)}) async-start(f32[8,16,128]{2,1,0:T(8,128)} %bitcast.5), calls=%async_computation.1 | async-start | bytes 131072 | tf_op jit(solution)/shard_map/all_to_all | solution.py:549
  37.0 1.9 %collective-permute-start.2 = (f32[64,128]{1,0:T(8,128)S(1)}, f32[64,128]{1,0:T(8,128)S(1)}, u32[]{:S(2)}, u32[]{:S(2)}) collective-permute-start(f32[64,128]{1,0:T(8,128)S(1)} %get-tuple-element.40), channel_id=1, source_target_pairs={{0,8},{8,16},{16,24},{24,32},{32,40},{40,48},{48,56},{56,64},{64,7... | collective-permute-start | bytes 98312 | tf_op jit(solution)/shard_map/ppermute | solution.py:552
  38.9 5.8 %collective-permute-start.3 = (f32[64,128]{1,0:T(8,128)S(1)}, f32[64,128]{1,0:T(8,128)S(1)}, u32[]{:S(2)}, u32[]{:S(2)}) collective-permute-start(f32[64,128]{1,0:T(8,128)S(1)} %get-tuple-element.41), channel_id=1, source_target_pairs={{8,0},{16,8},{24,16},{32,24},{40,32},{48,40},{56,48},{64,56},{72,6... | collective-permute-start | bytes 98312 | tf_op jit(solution)/shard_map/ppermute | solution.py:553
  44.7 0.0 collective-permute-done.2.from_left
  44.7 1.6 %collective-permute-done.3.from_right = f32[64,128]{1,0:T(8,128)S(1)} collective-permute-done((f32[64,128]{1,0:T(8,128)S(1)}, f32[64,128]{1,0:T(8,128)S(1)}, u32[]{:S(2)}, u32[]{:S(2)}) %collective-permute-start.3) | collective-permute-done | bytes 32800 | tf_op jit(solution)/shard_map/ppermute | solution.py:553
  46.3 0.0 all-to-all-done.1
  46.3 0.0 copy-start
  46.3 2.5 %next.3 = (f32[1024,128]{1,0:T(8,128)S(1)}, f32[64,128]{1,0:T(8,128)S(1)}, f32[64,128]{1,0:T(8,128)S(1)}, f32[64,128]{1,0:T(8,128)S(1)}, f32[128,128]{1,0:T(8,128)}) custom-call(s32[256]{0:T(256)S(1)} %get-tuple-element.27.slots.slots_any, f32[1024,128]{1,0:T(8,128)S(1)} %get-tuple-element.39.u_ref.first_ref, ...), custom_call_target="tpu_custom_call" | custom-call | tf_op jit(solution)/shard_map/next/pallas_call | solution.py:598
  48.8 7.2 %all-to-all-start.2 = ((f32[8,16,128]{2,1,0:T(8,128)}), f32[8,16,128]{2,1,0:T(8,128)S(1)}, u32[]{:S(2)}, u32[]{:S(2)}) async-start(f32[8,16,128]{2,1,0:T(8,128)} %bitcast.7), calls=%async_computation.2 | async-start | bytes 131072 | tf_op jit(solution)/shard_map/all_to_all | solution.py:549
  56.0 1.9 %collective-permute-start.4 = (f32[64,128]{1,0:T(8,128)S(1)}, f32[64,128]{1,0:T(8,128)S(1)}, u32[]{:S(2)}, u32[]{:S(2)}) collective-permute-start(f32[64,128]{1,0:T(8,128)S(1)} %get-tuple-element.45), channel_id=1, source_target_pairs={{0,8},{8,16},{16,24},{24,32},{32,40},{40,48},{48,56},{56,64},{64,7... | collective-permute-start | bytes 98312 | tf_op jit(solution)/shard_map/ppermute | solution.py:552
  57.9 5.8 %collective-permute-start.5 = (f32[64,128]{1,0:T(8,128)S(1)}, f32[64,128]{1,0:T(8,128)S(1)}, u32[]{:S(2)}, u32[]{:S(2)}) collective-permute-start(f32[64,128]{1,0:T(8,128)S(1)} %get-tuple-element.46), channel_id=1, source_target_pairs={{8,0},{16,8},{24,16},{32,24},{40,32},{48,40},{56,48},{64,56},{72,6... | collective-permute-start | bytes 98312 | tf_op jit(solution)/shard_map/ppermute | solution.py:553
  63.7 0.0 collective-permute-done.4.from_left
  63.7 1.6 %collective-permute-done.5.from_right = f32[64,128]{1,0:T(8,128)S(1)} collective-permute-done((f32[64,128]{1,0:T(8,128)S(1)}, f32[64,128]{1,0:T(8,128)S(1)}, u32[]{:S(2)}, u32[]{:S(2)}) %collective-permute-start.5) | collective-permute-done | bytes 32800 | tf_op jit(solution)/shard_map/ppermute | solution.py:553
  65.3 0.0 all-to-all-done.2
  65.3 0.0 copy-done
  65.3 2.3 %last.1 = f32[5,32,512]{2,1,0:T(8,128)} custom-call(s32[256]{0:T(256)S(1)} %get-tuple-element.27.slots.slots_any, f32[1024,128]{1,0:T(8,128)S(1)} %get-tuple-element.44.u_ref, f32[64,128]{1,0:T(8,128)S(1)} %collective-permute-done.4.from_left, f32[64,128]{1,0:T(8,128)S(1)} %collective-permute-done.5.from_right, f32[128,128]{1,0:T(8,128)S(1)} %bitcast.10, ...), custom_call_target="tpu_custom_call" | custom-call | tf_op jit(solution)/shard_map/last/pallas_call | solution.py:607
Async XLA Ops:
  2.8 24.8 %all-to-all-start = ((f32[8,16,128]{2,1,0:T(8,128)}), f32[8,16,128]{2,1,0:T(8,128)S(1)}, u32[]{:S(2)}, u32[]{:S(2)}) async-start(f32[8,16,128]{2,1,0:T(8,128)} %bitcast.3), calls=%async_computation | async-start | bytes 131072 | tf_op jit(solution)/shard_map/all_to_all | solution.py:549
  9.9 16.9 %collective-permute-start = (f32[64,128]{1,0:T(8,128)S(1)}, f32[64,128]{1,0:T(8,128)S(1)}, u32[]{:S(2)}, u32[]{:S(2)}) collective-permute-start(f32[64,128]{1,0:T(8,128)S(1)} %get-tuple-element.29), channel_id=1, source_target_pairs={{0,8},{8,16},{16,24},{24,32},{32,40},{40,48},{48,56},{56,64},{64,7... | collective-permute-start | bytes 98312 | tf_op jit(solution)/shard_map/ppermute | solution.py:552
  11.8 14.2 %copy-start.4 = (s32[32]{0:T(128)S(1)}, s32[32]{0:T(128)}, u32[]{:S(2)}) copy-start(s32[32]{0:T(128)} %levels.1) | copy-start | bytes 388
  11.8 14.2 %copy-start.1 = (s32[8]{0:T(128)S(1)}, s32[8]{0:T(128)}, u32[]{:S(2)}) copy-start(s32[8]{0:T(128)} %send_counts.1) | copy-start | bytes 100
  11.8 14.2 %copy-start.2 = (s32[8]{0:T(128)S(1)}, s32[8]{0:T(128)}, u32[]{:S(2)}) copy-start(s32[8]{0:T(128)} %recv_counts.1) | copy-start | bytes 100
  11.8 14.2 %copy-start.3 = (s32[2]{0:T(128)S(1)}, s32[2]{0:T(128)}, u32[]{:S(2)}) copy-start(s32[2]{0:T(128)} %curve_counts.1) | copy-start | bytes 28
  11.9 15.7 %collective-permute-start.1 = (f32[64,128]{1,0:T(8,128)S(1)}, f32[64,128]{1,0:T(8,128)S(1)}, u32[]{:S(2)}, u32[]{:S(2)}) collective-permute-start(f32[64,128]{1,0:T(8,128)S(1)} %get-tuple-element.30), channel_id=1, source_target_pairs={{8,0},{16,8},{24,16},{32,24},{40,32},{48,40},{56,48},{64,56},{72,6... | collective-permute-start | bytes 98312 | tf_op jit(solution)/shard_map/ppermute | solution.py:553
  30.1 16.2 %all-to-all-start.1 = ((f32[8,16,128]{2,1,0:T(8,128)}), f32[8,16,128]{2,1,0:T(8,128)S(1)}, u32[]{:S(2)}, u32[]{:S(2)}) async-start(f32[8,16,128]{2,1,0:T(8,128)} %bitcast.5), calls=%async_computation.1 | async-start | bytes 131072 | tf_op jit(solution)/shard_map/all_to_all | solution.py:549
  37.0 7.7 %collective-permute-start.2 = (f32[64,128]{1,0:T(8,128)S(1)}, f32[64,128]{1,0:T(8,128)S(1)}, u32[]{:S(2)}, u32[]{:S(2)}) collective-permute-start(f32[64,128]{1,0:T(8,128)S(1)} %get-tuple-element.40), channel_id=1, source_target_pairs={{0,8},{8,16},{16,24},{24,32},{32,40},{40,48},{48,56},{56,64},{64,7... | collective-permute-start | bytes 98312 | tf_op jit(solution)/shard_map/ppermute | solution.py:552
  38.9 7.3 %collective-permute-start.3 = (f32[64,128]{1,0:T(8,128)S(1)}, f32[64,128]{1,0:T(8,128)S(1)}, u32[]{:S(2)}, u32[]{:S(2)}) collective-permute-start(f32[64,128]{1,0:T(8,128)S(1)} %get-tuple-element.41), channel_id=1, source_target_pairs={{8,0},{16,8},{24,16},{32,24},{40,32},{48,40},{56,48},{64,56},{72,6... | collective-permute-start | bytes 98312 | tf_op jit(solution)/shard_map/ppermute | solution.py:553
  46.3 19.0 %copy-start = (f32[5,32,512]{2,1,0:T(8,128)S(1)}, f32[5,32,512]{2,1,0:T(8,128)}, u32[]{:S(2)}) copy-start(f32[5,32,512]{2,1,0:T(8,128)} %state_ref.1) | copy-start | bytes 983044
  48.8 16.5 %all-to-all-start.2 = ((f32[8,16,128]{2,1,0:T(8,128)}), f32[8,16,128]{2,1,0:T(8,128)S(1)}, u32[]{:S(2)}, u32[]{:S(2)}) async-start(f32[8,16,128]{2,1,0:T(8,128)} %bitcast.7), calls=%async_computation.2 | async-start | bytes 131072 | tf_op jit(solution)/shard_map/all_to_all | solution.py:549
  56.0 7.7 %collective-permute-start.4 = (f32[64,128]{1,0:T(8,128)S(1)}, f32[64,128]{1,0:T(8,128)S(1)}, u32[]{:S(2)}, u32[]{:S(2)}) collective-permute-start(f32[64,128]{1,0:T(8,128)S(1)} %get-tuple-element.45), channel_id=1, source_target_pairs={{0,8},{8,16},{16,24},{24,32},{32,40},{40,48},{48,56},{56,64},{64,7... | collective-permute-start | bytes 98312 | tf_op jit(solution)/shard_map/ppermute | solution.py:552
  57.9 7.3 %collective-permute-start.5 = (f32[64,128]{1,0:T(8,128)S(1)}, f32[64,128]{1,0:T(8,128)S(1)}, u32[]{:S(2)}, u32[]{:S(2)}) collective-permute-start(f32[64,128]{1,0:T(8,128)S(1)} %get-tuple-element.46), channel_id=1, source_target_pairs={{8,0},{16,8},{24,16},{32,24},{40,32},{48,40},{56,48},{64,56},{72,6... | collective-permute-start | bytes 98312 | tf_op jit(solution)/shard_map/ppermute | solution.py:553

commit v3 on v2

--- a/solution.py
+++ b/solution.py
@@ -187,7 +187,7 @@
             (sign * q[1] - q[4]) * scale,
         ]
         for f in range(5):
-            out_ref[pl.ds(f, 8, stride=8), :] = parts[f]
+            out_ref[8 * f : 8 * f + 8, :] = parts[f]
 
 
 def pack_tile(u_ref, slots, masks_ref, index_ref, mats_ref, tmp, own_ref, tile_ref, ready=None):
@@ -249,8 +249,10 @@
     for f in range(5):
         tmp[pl.ds(f, 8, stride=8), :] = q[f]
     for side, in_ref in ((0, from_left), (1, from_right)):
+        for f in range(5):
+            tmp[pl.ds(64 + 64 * side + f, 8, stride=8), :] = in_ref[8 * f : 8 * f + 8, :]
         for k in range(8):
-            pair = in_ref[8 * k : 8 * k + 8, :]
+            pair = tmp[64 + 64 * side + 8 * k : 72 + 64 * side + 8 * k, :]
             turned = pltpu.roll(pair, 64, 1)
             for s, value in ((k, (pair, turned)[side]), (k + 8, (turned, pair)[side])):
                 w_ref = w_refs[3 * side]
@@ -540,7 +542,7 @@
             **kwargs,
         )
 
-    payload = [shape(64, 128)] * 3 + [shape(128, 128)]
+    payload = [shape(40, 128)] * 2 + [shape(64, 128), shape(128, 128)]
     n_curve = lax.axis_size("curve")
     rightward = [(i, i + 1) for i in range(n_curve - 1)]
     leftward = [(i + 1, i) for i in range(n_curve - 1)]
@@ -573,7 +575,7 @@
         ],
     )(*[pltpu.with_memory_space_constraint(x, pltpu.HBM) for x in (state, *numbers, index, mats, coefs)])
     scratch = [pltpu.VMEM((256, 128), f32)] * 4
-    scratch += [pltpu.VMEM((128, 128), f32), pltpu.SMEM((256,), i32)]
+    scratch += [pltpu.VMEM((192, 128), f32), pltpu.SMEM((256,), i32)]
     sems = pltpu.SemaphoreType.DMA((2,))
     kept = []
     for section in range(3):

time: 68.5 us -> 68.2 us (level)
  no operation moved by 1% of the time
where the time goes in v3:
time: 68.2 us; the launch traced here: 67.2 us
  starting transfers between devices  52.6 us (77%)
  Pallas kernels  10.8 us (16%)
  waiting for transfers between devices  3.58 us (5%)
    ppermute x3, starting transfers between devices, exchange(): from_right = lax.ppermute(left, 'curve', leftward)  25.6 us
    all_to_all x3, starting transfers between devices, exchange(): lax.all_to_all(tile.reshape(8, 16, 128), 'tile', split_axis=0, concat_axi...  21.2 us
    ppermute x3, starting transfers between devices, exchange(): from_left = lax.ppermute(right, 'curve', rightward)  5.73 us
    pallas_call x2, Pallas kernels, shards(): call(next_kernel, 'next', out_shape=[shape(1024, 128), *payload], in_spec...  4.99 us
    ppermute x3, waiting for transfers between devices, exchange(): from_right = lax.ppermute(left, 'curve', leftward)  3.56 us
    pallas_call x1, Pallas kernels, shards(): call(first_kernel, 'first', out_shape=[shape(1024, 128), *payload, shape(...  2.76 us
    pallas_call x1, Pallas kernels, shards(): call(last_kernel, 'last', out_shape=shape(5, 32, 512), in_specs=[anywhere...  2.32 us
  transfers between devices with their start and end apart: 9, of which 3 were waited for; matrix products, arithmetic and copies ran while one was open for 0% of the time, Pallas kernels for 1%

profile of v3, /device:TPU:6, one launch (start us, length us, event | category | flops | bytes accessed | tf_op | source)
XLA Modules:
  0.0 67.2 jit_solution(16210498802151984947)
XLA Ops:
  0.0 2.8 %first.1 = (f32[1024,128]{1,0:T(8,128)S(1)}, f32[40,128]{1,0:T(8,128)S(1)}, f32[40,128]{1,0:T(8,128)S(1)}, f32[64,128]{1,0:T(8,128)S(1)}, f32[128,128]{1,0:T(8,1...) custom-call(f32[5,32,512]{2,1,0:T(8,128)} %state_ref.1, ...), custom_call_target="tpu_custom_call" | custom-call | tf_op jit(solution)/shard_map/first/pallas_call | solution.py:562
  2.8 7.1 %all-to-all-start = ((f32[8,16,128]{2,1,0:T(8,128)}), f32[8,16,128]{2,1,0:T(8,128)S(1)}, u32[]{:S(2)}, u32[]{:S(2)}) async-start(f32[8,16,128]{2,1,0:T(8,128)} %bitcast.3), calls=%async_computation | async-start | bytes 131072 | tf_op jit(solution)/shard_map/all_to_all | solution.py:551
  9.9 1.9 %collective-permute-start = (f32[40,128]{1,0:T(8,128)S(1)}, f32[40,128]{1,0:T(8,128)S(1)}, u32[]{:S(2)}, u32[]{:S(2)}) collective-permute-start(f32[40,128]{1,0:T(8,128)S(1)} %get-tuple-element.29), channel_id=1, source_target_pairs={{0,8},{8,16},{16,24},{24,32},{32,40},{40,48},{48,56},{56,64},{64,7... | collective-permute-start | bytes 61448 | tf_op jit(solution)/shard_map/ppermute | solution.py:554
  11.8 0.0 copy-start.4
  11.8 0.0 copy-start.1
  11.8 0.0 copy-start.2
  11.8 0.0 copy-start.3
  11.8 14.1 %collective-permute-start.1 = (f32[40,128]{1,0:T(8,128)S(1)}, f32[40,128]{1,0:T(8,128)S(1)}, u32[]{:S(2)}, u32[]{:S(2)}) collective-permute-start(f32[40,128]{1,0:T(8,128)S(1)} %get-tuple-element.30), channel_id=1, source_target_pairs={{8,0},{16,8},{24,16},{32,24},{40,32},{48,40},{56,48},{64,56},{72,6... | collective-permute-start | bytes 61448 | tf_op jit(solution)/shard_map/ppermute | solution.py:555
  26.0 0.0 copy-done.4
  26.0 0.0 copy-done.1
  26.0 0.0 copy-done.2
  26.0 0.0 copy-done.3
  26.0 0.7 %faces.1 = (f32[352,128]{1,0:T(8,128)S(1)}, f32[256,128]{1,0:T(8,128)S(1)}) custom-call(s32[256]{0:T(256)S(1)} %get-tuple-element.27.slots.slots_any, s32[32]{0:T(128)S(1)} %copy-done.4, s32[8]{0:T(128)S(1)} %copy-done.1, s32[8]{0:T(128)S(1)} %copy-done.2, s32[2]{0:T(128)S(1)} %copy-done.3), custom_call_target="tpu_custom_call" | custom-call | flops 20000000 | bytes 1000000 | tf_op jit(solution)/shard_map/faces/pallas_call | solution.py:584
  26.8 0.0 collective-permute-done.from_left
  26.8 0.7 collective-permute-done.1.from_right
  27.5 0.0 all-to-all-done
  27.5 2.5 %next.2 = (f32[1024,128]{1,0:T(8,128)S(1)}, f32[40,128]{1,0:T(8,128)S(1)}, f32[40,128]{1,0:T(8,128)S(1)}, f32[64,128]{1,0:T(8,128)S(1)}, f32[128,128]{1,0:T(8,128)}) custom-call(s32[256]{0:T(256)S(1)} %get-tuple-element.27.slots.slots_any, f32[1024,128]{1,0:T(8,128)S(1)} %get-tuple-element.28.u_ref, f32[40,128]{1,0:T(8,128)S(1)} %collective-permute-done.from_left, ...), custom_call_target="tpu_custom_call" | custom-call | tf_op jit(solution)/shard_map/next/pallas_call | solution.py:600
  30.0 6.9 %all-to-all-start.1 = ((f32[8,16,128]{2,1,0:T(8,128)}), f32[8,16,128]{2,1,0:T(8,128)S(1)}, u32[]{:S(2)}, u32[]{:S(2)}) async-start(f32[8,16,128]{2,1,0:T(8,128)} %bitcast.5), calls=%async_computation.1 | async-start | bytes 131072 | tf_op jit(solution)/shard_map/all_to_all | solution.py:551
  36.9 1.9 %collective-permute-start.2 = (f32[40,128]{1,0:T(8,128)S(1)}, f32[40,128]{1,0:T(8,128)S(1)}, u32[]{:S(2)}, u32[]{:S(2)}) collective-permute-start(f32[40,128]{1,0:T(8,128)S(1)} %get-tuple-element.40), channel_id=1, source_target_pairs={{0,8},{8,16},{16,24},{24,32},{32,40},{40,48},{48,56},{56,64},{64,7... | collective-permute-start | bytes 61448 | tf_op jit(solution)/shard_map/ppermute | solution.py:554
  38.8 5.8 %collective-permute-start.3 = (f32[40,128]{1,0:T(8,128)S(1)}, f32[40,128]{1,0:T(8,128)S(1)}, u32[]{:S(2)}, u32[]{:S(2)}) collective-permute-start(f32[40,128]{1,0:T(8,128)S(1)} %get-tuple-element.41), channel_id=1, source_target_pairs={{8,0},{16,8},{24,16},{32,24},{40,32},{48,40},{56,48},{64,56},{72,6... | collective-permute-start | bytes 61448 | tf_op jit(solution)/shard_map/ppermute | solution.py:555
  44.6 0.0 collective-permute-done.2.from_left
  44.6 1.4 %collective-permute-done.3.from_right = f32[40,128]{1,0:T(8,128)S(1)} collective-permute-done((f32[40,128]{1,0:T(8,128)S(1)}, f32[40,128]{1,0:T(8,128)S(1)}, u32[]{:S(2)}, u32[]{:S(2)}) %collective-permute-start.3) | collective-permute-done | bytes 20512 | tf_op jit(solution)/shard_map/ppermute | solution.py:555
  46.0 0.0 all-to-all-done.1
  46.0 0.0 copy-start
  46.0 2.5 %next.3 = (f32[1024,128]{1,0:T(8,128)S(1)}, f32[40,128]{1,0:T(8,128)S(1)}, f32[40,128]{1,0:T(8,128)S(1)}, f32[64,128]{1,0:T(8,128)S(1)}, f32[128,128]{1,0:T(8,128)}) custom-call(s32[256]{0:T(256)S(1)} %get-tuple-element.27.slots.slots_any, f32[1024,128]{1,0:T(8,128)S(1)} %get-tuple-element.39.u_ref.first_ref, ...), custom_call_target="tpu_custom_call" | custom-call | tf_op jit(solution)/shard_map/next/pallas_call | solution.py:600
  48.5 7.2 %all-to-all-start.2 = ((f32[8,16,128]{2,1,0:T(8,128)}), f32[8,16,128]{2,1,0:T(8,128)S(1)}, u32[]{:S(2)}, u32[]{:S(2)}) async-start(f32[8,16,128]{2,1,0:T(8,128)} %bitcast.7), calls=%async_computation.2 | async-start | bytes 131072 | tf_op jit(solution)/shard_map/all_to_all | solution.py:551
  55.7 1.9 %collective-permute-start.4 = (f32[40,128]{1,0:T(8,128)S(1)}, f32[40,128]{1,0:T(8,128)S(1)}, u32[]{:S(2)}, u32[]{:S(2)}) collective-permute-start(f32[40,128]{1,0:T(8,128)S(1)} %get-tuple-element.45), channel_id=1, source_target_pairs={{0,8},{8,16},{16,24},{24,32},{32,40},{40,48},{48,56},{56,64},{64,7... | collective-permute-start | bytes 61448 | tf_op jit(solution)/shard_map/ppermute | solution.py:554
  57.6 5.8 %collective-permute-start.5 = (f32[40,128]{1,0:T(8,128)S(1)}, f32[40,128]{1,0:T(8,128)S(1)}, u32[]{:S(2)}, u32[]{:S(2)}) collective-permute-start(f32[40,128]{1,0:T(8,128)S(1)} %get-tuple-element.46), channel_id=1, source_target_pairs={{8,0},{16,8},{24,16},{32,24},{40,32},{48,40},{56,48},{64,56},{72,6... | collective-permute-start | bytes 61448 | tf_op jit(solution)/shard_map/ppermute | solution.py:555
  63.4 0.0 collective-permute-done.4.from_left
  63.4 1.4 %collective-permute-done.5.from_right = f32[40,128]{1,0:T(8,128)S(1)} collective-permute-done((f32[40,128]{1,0:T(8,128)S(1)}, f32[40,128]{1,0:T(8,128)S(1)}, u32[]{:S(2)}, u32[]{:S(2)}) %collective-permute-start.5) | collective-permute-done | bytes 20512 | tf_op jit(solution)/shard_map/ppermute | solution.py:555
  64.9 0.0 all-to-all-done.2
  64.9 0.0 copy-done
  64.9 2.3 %last.1 = f32[5,32,512]{2,1,0:T(8,128)} custom-call(s32[256]{0:T(256)S(1)} %get-tuple-element.27.slots.slots_any, f32[1024,128]{1,0:T(8,128)S(1)} %get-tuple-element.44.u_ref, f32[40,128]{1,0:T(8,128)S(1)} %collective-permute-done.4.from_left, f32[40,128]{1,0:T(8,128)S(1)} %collective-permute-done.5.from_right, f32[128,128]{1,0:T(8,128)S(1)} %bitcast.10, ...), custom_call_target="tpu_custom_call" | custom-call | tf_op jit(solution)/shard_map/last/pallas_call | solution.py:609
Async XLA Ops:
  2.8 24.7 %all-to-all-start = ((f32[8,16,128]{2,1,0:T(8,128)}), f32[8,16,128]{2,1,0:T(8,128)S(1)}, u32[]{:S(2)}, u32[]{:S(2)}) async-start(f32[8,16,128]{2,1,0:T(8,128)} %bitcast.3), calls=%async_computation | async-start | bytes 131072 | tf_op jit(solution)/shard_map/all_to_all | solution.py:551
  9.9 16.9 %collective-permute-start = (f32[40,128]{1,0:T(8,128)S(1)}, f32[40,128]{1,0:T(8,128)S(1)}, u32[]{:S(2)}, u32[]{:S(2)}) collective-permute-start(f32[40,128]{1,0:T(8,128)S(1)} %get-tuple-element.29), channel_id=1, source_target_pairs={{0,8},{8,16},{16,24},{24,32},{32,40},{40,48},{48,56},{56,64},{64,7... | collective-permute-start | bytes 61448 | tf_op jit(solution)/shard_map/ppermute | solution.py:554
  11.8 14.2 %copy-start.4 = (s32[32]{0:T(128)S(1)}, s32[32]{0:T(128)}, u32[]{:S(2)}) copy-start(s32[32]{0:T(128)} %levels.1) | copy-start | bytes 388
  11.8 14.2 %copy-start.1 = (s32[8]{0:T(128)S(1)}, s32[8]{0:T(128)}, u32[]{:S(2)}) copy-start(s32[8]{0:T(128)} %send_counts.1) | copy-start | bytes 100
  11.8 14.2 %copy-start.2 = (s32[8]{0:T(128)S(1)}, s32[8]{0:T(128)}, u32[]{:S(2)}) copy-start(s32[8]{0:T(128)} %recv_counts.1) | copy-start | bytes 100
  11.8 14.2 %copy-start.3 = (s32[2]{0:T(128)S(1)}, s32[2]{0:T(128)}, u32[]{:S(2)}) copy-start(s32[2]{0:T(128)} %curve_counts.1) | copy-start | bytes 28
  11.8 15.6 %collective-permute-start.1 = (f32[40,128]{1,0:T(8,128)S(1)}, f32[40,128]{1,0:T(8,128)S(1)}, u32[]{:S(2)}, u32[]{:S(2)}) collective-permute-start(f32[40,128]{1,0:T(8,128)S(1)} %get-tuple-element.30), channel_id=1, source_target_pairs={{8,0},{16,8},{24,16},{32,24},{40,32},{48,40},{56,48},{64,56},{72,6... | collective-permute-start | bytes 61448 | tf_op jit(solution)/shard_map/ppermute | solution.py:555
  30.0 16.1 %all-to-all-start.1 = ((f32[8,16,128]{2,1,0:T(8,128)}), f32[8,16,128]{2,1,0:T(8,128)S(1)}, u32[]{:S(2)}, u32[]{:S(2)}) async-start(f32[8,16,128]{2,1,0:T(8,128)} %bitcast.5), calls=%async_computation.1 | async-start | bytes 131072 | tf_op jit(solution)/shard_map/all_to_all | solution.py:551
  36.9 7.7 %collective-permute-start.2 = (f32[40,128]{1,0:T(8,128)S(1)}, f32[40,128]{1,0:T(8,128)S(1)}, u32[]{:S(2)}, u32[]{:S(2)}) collective-permute-start(f32[40,128]{1,0:T(8,128)S(1)} %get-tuple-element.40), channel_id=1, source_target_pairs={{0,8},{8,16},{16,24},{24,32},{32,40},{40,48},{48,56},{56,64},{64,7... | collective-permute-start | bytes 61448 | tf_op jit(solution)/shard_map/ppermute | solution.py:554
  38.8 7.2 %collective-permute-start.3 = (f32[40,128]{1,0:T(8,128)S(1)}, f32[40,128]{1,0:T(8,128)S(1)}, u32[]{:S(2)}, u32[]{:S(2)}) collective-permute-start(f32[40,128]{1,0:T(8,128)S(1)} %get-tuple-element.41), channel_id=1, source_target_pairs={{8,0},{16,8},{24,16},{32,24},{40,32},{48,40},{56,48},{64,56},{72,6... | collective-permute-start | bytes 61448 | tf_op jit(solution)/shard_map/ppermute | solution.py:555
  46.0 18.8 %copy-start = (f32[5,32,512]{2,1,0:T(8,128)S(1)}, f32[5,32,512]{2,1,0:T(8,128)}, u32[]{:S(2)}) copy-start(f32[5,32,512]{2,1,0:T(8,128)} %state_ref.1) | copy-start | bytes 983044
  48.5 16.3 %all-to-all-start.2 = ((f32[8,16,128]{2,1,0:T(8,128)}), f32[8,16,128]{2,1,0:T(8,128)S(1)}, u32[]{:S(2)}, u32[]{:S(2)}) async-start(f32[8,16,128]{2,1,0:T(8,128)} %bitcast.7), calls=%async_computation.2 | async-start | bytes 131072 | tf_op jit(solution)/shard_map/all_to_all | solution.py:551
  55.7 7.7 %collective-permute-start.4 = (f32[40,128]{1,0:T(8,128)S(1)}, f32[40,128]{1,0:T(8,128)S(1)}, u32[]{:S(2)}, u32[]{:S(2)}) collective-permute-start(f32[40,128]{1,0:T(8,128)S(1)} %get-tuple-element.45), channel_id=1, source_target_pairs={{0,8},{8,16},{16,24},{24,32},{32,40},{40,48},{48,56},{56,64},{64,7... | collective-permute-start | bytes 61448 | tf_op jit(solution)/shard_map/ppermute | solution.py:554
  57.6 7.2 %collective-permute-start.5 = (f32[40,128]{1,0:T(8,128)S(1)}, f32[40,128]{1,0:T(8,128)S(1)}, u32[]{:S(2)}, u32[]{:S(2)}) collective-permute-start(f32[40,128]{1,0:T(8,128)S(1)} %get-tuple-element.46), channel_id=1, source_target_pairs={{8,0},{16,8},{24,16},{32,24},{40,32},{48,40},{56,48},{64,56},{72,6... | collective-permute-start | bytes 61448 | tf_op jit(solution)/shard_map/ppermute | solution.py:555

commit v4 on v3

--- a/solution.py
+++ b/solution.py
@@ -239,7 +239,7 @@
         w_refs[a][block, :] = w_refs[a][block, :] - jnp.where(at_face, moved, 0.0)
 
 
-def unpack(w_refs, slots, masks_ref, index_ref, mats_ref, tmp, from_left, from_right, tile_ref, own_ref):
+def unpack(w_refs, slots, masks_ref, index_ref, mats_ref, tmp, from_left, from_right, tile_ref, own_ref, ready):
     low = lanes() < 64
     q = [
         tile_ref[pl.ds(8 + f, 8, stride=16), :] - own_ref[pl.ds(f, 8, stride=8), :]
@@ -251,6 +251,8 @@
     for side, in_ref in ((0, from_left), (1, from_right)):
         for f in range(5):
             tmp[pl.ds(64 + 64 * side + f, 8, stride=8), :] = in_ref[8 * f : 8 * f + 8, :]
+    ready.wait()
+    for side in range(2):
         for k in range(8):
             pair = tmp[64 + 64 * side + 8 * k : 72 + 64 * side + 8 * k, :]
             turned = pltpu.roll(pair, 64, 1)
@@ -482,9 +484,9 @@
     fetch = pltpu.make_async_copy(slots_any, slots, sems.at[0])
     fetch.start()
     inside(u_ref, faces_ref, mats_ref, coefs_ref, w_refs)
-    fetch.wait()
     unpack(
-        w_refs, slots, masks_ref, index_ref, mats_ref, tmp, from_left, from_right, arrived_ref, sent_ref
+        w_refs, slots, masks_ref, index_ref, mats_ref, tmp, from_left, from_right, arrived_ref, sent_ref,
+        fetch,
     )
     for a in range(4):
         out_ref[256 * a : 256 * a + 256, :] = w_refs[a][...] * scale_ref[...]
@@ -504,9 +506,9 @@
     fetch = pltpu.make_async_copy(slots_any, slots, sems.at[0])
     fetch.start()
     inside(u_ref, faces_ref, mats_ref, coefs_ref, w_refs)
-    fetch.wait()
     unpack(
-        w_refs, slots, masks_ref, index_ref, mats_ref, tmp, from_left, from_right, arrived_ref, sent_ref
+        w_refs, slots, masks_ref, index_ref, mats_ref, tmp, from_left, from_right, arrived_ref, sent_ref,
+        fetch,
     )
     scale = scale_ref[pl.ds(0, 32, stride=8), :] * (1.0 / 6.0)
     for f in range(5):

time: 68.2 us -> 68.3 us (level)
  no operation moved by 1% of the time
where the time goes in v4:
time: 68.3 us; the launch traced here: 67.2 us
  starting transfers between devices  52.7 us (77%)
  Pallas kernels  10.8 us (16%)
  waiting for transfers between devices  3.58 us (5%)
    ppermute x3, starting transfers between devices, exchange(): from_right = lax.ppermute(left, 'curve', leftward)  25.6 us
    all_to_all x3, starting transfers between devices, exchange(): lax.all_to_all(tile.reshape(8, 16, 128), 'tile', split_axis=0, concat_axi...  21.3 us
    ppermute x3, starting transfers between devices, exchange(): from_left = lax.ppermute(right, 'curve', rightward)  5.73 us
    pallas_call x2, Pallas kernels, shards(): call(next_kernel, 'next', out_shape=[shape(1024, 128), *payload], in_spec...  4.93 us
    ppermute x3, waiting for transfers between devices, exchange(): from_right = lax.ppermute(left, 'curve', leftward)  3.56 us
    pallas_call x1, Pallas kernels, shards(): call(first_kernel, 'first', out_shape=[shape(1024, 128), *payload, shape(...  2.76 us
    pallas_call x1, Pallas kernels, shards(): call(last_kernel, 'last', out_shape=shape(5, 32, 512), in_specs=[anywhere...  2.36 us
  transfers between devices with their start and end apart: 9, of which 3 were waited for; matrix products, arithmetic and copies ran while one was open for 0% of the time, Pallas kernels for 1%

profile of v4, /device:TPU:6, one launch (start us, length us, event | category | flops | bytes accessed | tf_op | source)
XLA Modules:
  0.0 67.2 jit_solution(5341082439227613119)
XLA Ops:
  0.0 2.8 %first.1 = (f32[1024,128]{1,0:T(8,128)S(1)}, f32[40,128]{1,0:T(8,128)S(1)}, f32[40,128]{1,0:T(8,128)S(1)}, f32[64,128]{1,0:T(8,128)S(1)}, f32[128,128]{1,0:T(8,1...) custom-call(f32[5,32,512]{2,1,0:T(8,128)} %state_ref.1, ...), custom_call_target="tpu_custom_call" | custom-call | tf_op jit(solution)/shard_map/first/pallas_call | solution.py:564
  2.8 7.1 %all-to-all-start = ((f32[8,16,128]{2,1,0:T(8,128)}), f32[8,16,128]{2,1,0:T(8,128)S(1)}, u32[]{:S(2)}, u32[]{:S(2)}) async-start(f32[8,16,128]{2,1,0:T(8,128)} %bitcast.3), calls=%async_computation | async-start | bytes 131072 | tf_op jit(solution)/shard_map/all_to_all | solution.py:553
  9.9 1.9 %collective-permute-start = (f32[40,128]{1,0:T(8,128)S(1)}, f32[40,128]{1,0:T(8,128)S(1)}, u32[]{:S(2)}, u32[]{:S(2)}) collective-permute-start(f32[40,128]{1,0:T(8,128)S(1)} %get-tuple-element.29), channel_id=1, source_target_pairs={{0,8},{8,16},{16,24},{24,32},{32,40},{40,48},{48,56},{56,64},{64,7... | collective-permute-start | bytes 61448 | tf_op jit(solution)/shard_map/ppermute | solution.py:556
  11.8 0.0 copy-start.4
  11.8 0.0 copy-start.1
  11.8 0.0 copy-start.2
  11.8 0.0 copy-start.3
  11.9 14.1 %collective-permute-start.1 = (f32[40,128]{1,0:T(8,128)S(1)}, f32[40,128]{1,0:T(8,128)S(1)}, u32[]{:S(2)}, u32[]{:S(2)}) collective-permute-start(f32[40,128]{1,0:T(8,128)S(1)} %get-tuple-element.30), channel_id=1, source_target_pairs={{8,0},{16,8},{24,16},{32,24},{40,32},{48,40},{56,48},{64,56},{72,6... | collective-permute-start | bytes 61448 | tf_op jit(solution)/shard_map/ppermute | solution.py:557
  26.0 0.0 copy-done.4
  26.0 0.0 copy-done.1
  26.0 0.0 copy-done.2
  26.0 0.0 copy-done.3
  26.0 0.7 %faces.1 = (f32[352,128]{1,0:T(8,128)S(1)}, f32[256,128]{1,0:T(8,128)S(1)}) custom-call(s32[256]{0:T(256)S(1)} %get-tuple-element.27.slots.slots_any, s32[32]{0:T(128)S(1)} %copy-done.4, s32[8]{0:T(128)S(1)} %copy-done.1, s32[8]{0:T(128)S(1)} %copy-done.2, s32[2]{0:T(128)S(1)} %copy-done.3), custom_call_target="tpu_custom_call" | custom-call | flops 20000000 | bytes 1000000 | tf_op jit(solution)/shard_map/faces/pallas_call | solution.py:586
  26.8 0.0 collective-permute-done.from_left
  26.8 0.7 collective-permute-done.1.from_right
  27.5 0.0 all-to-all-done
  27.5 2.5 %next.2 = (f32[1024,128]{1,0:T(8,128)S(1)}, f32[40,128]{1,0:T(8,128)S(1)}, f32[40,128]{1,0:T(8,128)S(1)}, f32[64,128]{1,0:T(8,128)S(1)}, f32[128,128]{1,0:T(8,128)}) custom-call(s32[256]{0:T(256)S(1)} %get-tuple-element.27.slots.slots_any, f32[1024,128]{1,0:T(8,128)S(1)} %get-tuple-element.28.u_ref, f32[40,128]{1,0:T(8,128)S(1)} %collective-permute-done.from_left, ...), custom_call_target="tpu_custom_call" | custom-call | tf_op jit(solution)/shard_map/next/pallas_call | solution.py:602
  29.9 7.0 %all-to-all-start.1 = ((f32[8,16,128]{2,1,0:T(8,128)}), f32[8,16,128]{2,1,0:T(8,128)S(1)}, u32[]{:S(2)}, u32[]{:S(2)}) async-start(f32[8,16,128]{2,1,0:T(8,128)} %bitcast.5), calls=%async_computation.1 | async-start | bytes 131072 | tf_op jit(solution)/shard_map/all_to_all | solution.py:553
  36.9 1.9 %collective-permute-start.2 = (f32[40,128]{1,0:T(8,128)S(1)}, f32[40,128]{1,0:T(8,128)S(1)}, u32[]{:S(2)}, u32[]{:S(2)}) collective-permute-start(f32[40,128]{1,0:T(8,128)S(1)} %get-tuple-element.40), channel_id=1, source_target_pairs={{0,8},{8,16},{16,24},{24,32},{32,40},{40,48},{48,56},{56,64},{64,7... | collective-permute-start | bytes 61448 | tf_op jit(solution)/shard_map/ppermute | solution.py:556
  38.8 5.8 %collective-permute-start.3 = (f32[40,128]{1,0:T(8,128)S(1)}, f32[40,128]{1,0:T(8,128)S(1)}, u32[]{:S(2)}, u32[]{:S(2)}) collective-permute-start(f32[40,128]{1,0:T(8,128)S(1)} %get-tuple-element.41), channel_id=1, source_target_pairs={{8,0},{16,8},{24,16},{32,24},{40,32},{48,40},{56,48},{64,56},{72,6... | collective-permute-start | bytes 61448 | tf_op jit(solution)/shard_map/ppermute | solution.py:557
  44.6 0.0 collective-permute-done.2.from_left
  44.6 1.4 %collective-permute-done.3.from_right = f32[40,128]{1,0:T(8,128)S(1)} collective-permute-done((f32[40,128]{1,0:T(8,128)S(1)}, f32[40,128]{1,0:T(8,128)S(1)}, u32[]{:S(2)}, u32[]{:S(2)}) %collective-permute-start.3) | collective-permute-done | bytes 20512 | tf_op jit(solution)/shard_map/ppermute | solution.py:557
  46.0 0.0 all-to-all-done.1
  46.0 0.0 copy-start
  46.0 2.5 %next.3 = (f32[1024,128]{1,0:T(8,128)S(1)}, f32[40,128]{1,0:T(8,128)S(1)}, f32[40,128]{1,0:T(8,128)S(1)}, f32[64,128]{1,0:T(8,128)S(1)}, f32[128,128]{1,0:T(8,128)}) custom-call(s32[256]{0:T(256)S(1)} %get-tuple-element.27.slots.slots_any, f32[1024,128]{1,0:T(8,128)S(1)} %get-tuple-element.39.u_ref.first_ref, ...), custom_call_target="tpu_custom_call" | custom-call | tf_op jit(solution)/shard_map/next/pallas_call | solution.py:602
  48.5 7.2 %all-to-all-start.2 = ((f32[8,16,128]{2,1,0:T(8,128)}), f32[8,16,128]{2,1,0:T(8,128)S(1)}, u32[]{:S(2)}, u32[]{:S(2)}) async-start(f32[8,16,128]{2,1,0:T(8,128)} %bitcast.7), calls=%async_computation.2 | async-start | bytes 131072 | tf_op jit(solution)/shard_map/all_to_all | solution.py:553
  55.7 1.9 %collective-permute-start.4 = (f32[40,128]{1,0:T(8,128)S(1)}, f32[40,128]{1,0:T(8,128)S(1)}, u32[]{:S(2)}, u32[]{:S(2)}) collective-permute-start(f32[40,128]{1,0:T(8,128)S(1)} %get-tuple-element.45), channel_id=1, source_target_pairs={{0,8},{8,16},{16,24},{24,32},{32,40},{40,48},{48,56},{56,64},{64,7... | collective-permute-start | bytes 61448 | tf_op jit(solution)/shard_map/ppermute | solution.py:556
  57.7 5.8 %collective-permute-start.5 = (f32[40,128]{1,0:T(8,128)S(1)}, f32[40,128]{1,0:T(8,128)S(1)}, u32[]{:S(2)}, u32[]{:S(2)}) collective-permute-start(f32[40,128]{1,0:T(8,128)S(1)} %get-tuple-element.46), channel_id=1, source_target_pairs={{8,0},{16,8},{24,16},{32,24},{40,32},{48,40},{56,48},{64,56},{72,6... | collective-permute-start | bytes 61448 | tf_op jit(solution)/shard_map/ppermute | solution.py:557
  63.4 0.0 collective-permute-done.4.from_left
  63.4 1.4 %collective-permute-done.5.from_right = f32[40,128]{1,0:T(8,128)S(1)} collective-permute-done((f32[40,128]{1,0:T(8,128)S(1)}, f32[40,128]{1,0:T(8,128)S(1)}, u32[]{:S(2)}, u32[]{:S(2)}) %collective-permute-start.5) | collective-permute-done | bytes 20512 | tf_op jit(solution)/shard_map/ppermute | solution.py:557
  64.9 0.0 all-to-all-done.2
  64.9 0.0 copy-done
  64.9 2.4 %last.1 = f32[5,32,512]{2,1,0:T(8,128)} custom-call(s32[256]{0:T(256)S(1)} %get-tuple-element.27.slots.slots_any, f32[1024,128]{1,0:T(8,128)S(1)} %get-tuple-element.44.u_ref, f32[40,128]{1,0:T(8,128)S(1)} %collective-permute-done.4.from_left, f32[40,128]{1,0:T(8,128)S(1)} %collective-permute-done.5.from_right, f32[128,128]{1,0:T(8,128)S(1)} %bitcast.10, ...), custom_call_target="tpu_custom_call" | custom-call | tf_op jit(solution)/shard_map/last/pallas_call | solution.py:611
Async XLA Ops:
  2.8 24.7 %all-to-all-start = ((f32[8,16,128]{2,1,0:T(8,128)}), f32[8,16,128]{2,1,0:T(8,128)S(1)}, u32[]{:S(2)}, u32[]{:S(2)}) async-start(f32[8,16,128]{2,1,0:T(8,128)} %bitcast.3), calls=%async_computation | async-start | bytes 131072 | tf_op jit(solution)/shard_map/all_to_all | solution.py:553
  9.9 16.9 %collective-permute-start = (f32[40,128]{1,0:T(8,128)S(1)}, f32[40,128]{1,0:T(8,128)S(1)}, u32[]{:S(2)}, u32[]{:S(2)}) collective-permute-start(f32[40,128]{1,0:T(8,128)S(1)} %get-tuple-element.29), channel_id=1, source_target_pairs={{0,8},{8,16},{16,24},{24,32},{32,40},{40,48},{48,56},{56,64},{64,7... | collective-permute-start | bytes 61448 | tf_op jit(solution)/shard_map/ppermute | solution.py:556
  11.8 14.2 %copy-start.4 = (s32[32]{0:T(128)S(1)}, s32[32]{0:T(128)}, u32[]{:S(2)}) copy-start(s32[32]{0:T(128)} %levels.1) | copy-start | bytes 388
  11.8 14.2 %copy-start.1 = (s32[8]{0:T(128)S(1)}, s32[8]{0:T(128)}, u32[]{:S(2)}) copy-start(s32[8]{0:T(128)} %send_counts.1) | copy-start | bytes 100
  11.8 14.2 %copy-start.2 = (s32[8]{0:T(128)S(1)}, s32[8]{0:T(128)}, u32[]{:S(2)}) copy-start(s32[8]{0:T(128)} %recv_counts.1) | copy-start | bytes 100
  11.8 14.2 %copy-start.3 = (s32[2]{0:T(128)S(1)}, s32[2]{0:T(128)}, u32[]{:S(2)}) copy-start(s32[2]{0:T(128)} %curve_counts.1) | copy-start | bytes 28
  11.9 15.6 %collective-permute-start.1 = (f32[40,128]{1,0:T(8,128)S(1)}, f32[40,128]{1,0:T(8,128)S(1)}, u32[]{:S(2)}, u32[]{:S(2)}) collective-permute-start(f32[40,128]{1,0:T(8,128)S(1)} %get-tuple-element.30), channel_id=1, source_target_pairs={{8,0},{16,8},{24,16},{32,24},{40,32},{48,40},{56,48},{64,56},{72,6... | collective-permute-start | bytes 61448 | tf_op jit(solution)/shard_map/ppermute | solution.py:557
  29.9 16.1 %all-to-all-start.1 = ((f32[8,16,128]{2,1,0:T(8,128)}), f32[8,16,128]{2,1,0:T(8,128)S(1)}, u32[]{:S(2)}, u32[]{:S(2)}) async-start(f32[8,16,128]{2,1,0:T(8,128)} %bitcast.5), calls=%async_computation.1 | async-start | bytes 131072 | tf_op jit(solution)/shard_map/all_to_all | solution.py:553
  36.9 7.7 %collective-permute-start.2 = (f32[40,128]{1,0:T(8,128)S(1)}, f32[40,128]{1,0:T(8,128)S(1)}, u32[]{:S(2)}, u32[]{:S(2)}) collective-permute-start(f32[40,128]{1,0:T(8,128)S(1)} %get-tuple-element.40), channel_id=1, source_target_pairs={{0,8},{8,16},{16,24},{24,32},{32,40},{40,48},{48,56},{56,64},{64,7... | collective-permute-start | bytes 61448 | tf_op jit(solution)/shard_map/ppermute | solution.py:556
  38.8 7.2 %collective-permute-start.3 = (f32[40,128]{1,0:T(8,128)S(1)}, f32[40,128]{1,0:T(8,128)S(1)}, u32[]{:S(2)}, u32[]{:S(2)}) collective-permute-start(f32[40,128]{1,0:T(8,128)S(1)} %get-tuple-element.41), channel_id=1, source_target_pairs={{8,0},{16,8},{24,16},{32,24},{40,32},{48,40},{56,48},{64,56},{72,6... | collective-permute-start | bytes 61448 | tf_op jit(solution)/shard_map/ppermute | solution.py:557
  46.0 18.9 %copy-start = (f32[5,32,512]{2,1,0:T(8,128)S(1)}, f32[5,32,512]{2,1,0:T(8,128)}, u32[]{:S(2)}) copy-start(f32[5,32,512]{2,1,0:T(8,128)} %state_ref.1) | copy-start | bytes 983044
  48.5 16.4 %all-to-all-start.2 = ((f32[8,16,128]{2,1,0:T(8,128)}), f32[8,16,128]{2,1,0:T(8,128)S(1)}, u32[]{:S(2)}, u32[]{:S(2)}) async-start(f32[8,16,128]{2,1,0:T(8,128)} %bitcast.7), calls=%async_computation.2 | async-start | bytes 131072 | tf_op jit(solution)/shard_map/all_to_all | solution.py:553
  55.7 7.7 %collective-permute-start.4 = (f32[40,128]{1,0:T(8,128)S(1)}, f32[40,128]{1,0:T(8,128)S(1)}, u32[]{:S(2)}, u32[]{:S(2)}) collective-permute-start(f32[40,128]{1,0:T(8,128)S(1)} %get-tuple-element.45), channel_id=1, source_target_pairs={{0,8},{8,16},{16,24},{24,32},{32,40},{40,48},{48,56},{56,64},{64,7... | collective-permute-start | bytes 61448 | tf_op jit(solution)/shard_map/ppermute | solution.py:556
  57.7 7.2 %collective-permute-start.5 = (f32[40,128]{1,0:T(8,128)S(1)}, f32[40,128]{1,0:T(8,128)S(1)}, u32[]{:S(2)}, u32[]{:S(2)}) collective-permute-start(f32[40,128]{1,0:T(8,128)S(1)} %get-tuple-element.46), channel_id=1, source_target_pairs={{8,0},{16,8},{24,16},{32,24},{40,32},{48,40},{56,48},{64,56},{72,6... | collective-permute-start | bytes 61448 | tf_op jit(solution)/shard_map/ppermute | solution.py:557
